TPU v7x, 512 devices: a whole 4x8x8 slice. The times are simulated.
512 devices in a mesh: light: 8 (over y), view: 64 (over z, x, core).
Axes of the slice: x: 4, y: 8, z: 8, core: 2. Of those that a mesh axis runs over, the one named last changes fastest.
Arguments:
- density: bfloat16 [32, 1024, 2048], P('light', 'view'), may hold values from 0 to 1
- occupied: int32 [8, 64, 16], P('light', 'view'), may hold values from 0 to 1, as said below
- view_sign: float32 [1], replicated, may hold values from -1 to 1, as said below
- transfer: float32 [4, 4], replicated, may hold values from -3 to 3
- absorb: float32 [3], replicated, may hold values from 0.5 to 20
- light_in: float32 [3, 1024, 2048], P(None, 'view'), may hold values from 1 to 2.5
Outputs:
- image: float32 [4, 65536], P(None, ('light', 'view'))
Inputs may be any that keep to these rules, and one draw needn't show every extreme that they name: `occupied`: 0 or 1; the share of occupied bricks differs from device to device. `view_sign`: magnitude 0.5 or more; either sign.
All inputs are finite; a program needn't handle non-finite values.
Results may differ from a plain program's by a relative error of at most 0.0003.
Values may be sent and summed in bfloat16 or wider, within the bound.
No kernel may reach another device: no remote copies, remote signals or barrier semaphores. Data moves between devices by JAX's collectives and lax.ppermute only.
A program may use at most 64 MiB of HBM per device.

v0:
```python
import jax
import jax.numpy as jnp
from jax import lax
from jax.sharding import PartitionSpec as P


def with_halo(cells, sides, width):
    for axis, dim in sides:
        count = lax.axis_size(axis)
        ends = count - 1
        head = lax.slice_in_dim(cells, 0, width, axis=dim)
        tail = lax.slice_in_dim(cells, cells.shape[dim] - width, cells.shape[dim], axis=dim)
        cells = jnp.concatenate(
            [
                lax.ppermute(tail, axis, [(i, (i + 1) % count) for i in range(ends)]),
                cells,
                lax.ppermute(head, axis, [((i + 1) % count, i) for i in range(ends)]),
            ],
            axis=dim,
        )
    return cells


def from_behind(x, axis, by):
    length = lax.axis_size(axis)
    pairs = [(i, i + by) for i in range(length) if 0 <= i + by < length]
    return lax.ppermute(x, axis, pairs)


def from_partner(value, axis, stride):
    mask = 2**stride
    pairs = [(source, source ^ mask) for source in range(lax.axis_size(axis))]
    return lax.ppermute(value, axis, pairs)


def polynomial(coeffs, values):
    return coeffs[0] + values * (coeffs[1] + values * (coeffs[2] + values * coeffs[3]))


def blur_columns(field):
    widths = [(0, 0)] * (field.ndim - 1) + [(1, 1)]
    padded = jnp.pad(field, widths)
    return 0.25 * padded[..., :-2] + 0.5 * padded[..., 1:-1] + 0.25 * padded[..., 2:]


def composite_depth(emitted, opacity, facing_back):
    emitted = jnp.where(facing_back == 1, jnp.flip(emitted, 1), emitted)
    opacity = jnp.where(facing_back == 1, jnp.flip(opacity, 0), opacity)
    passing = 1.0 - opacity
    through = jnp.cumprod(passing, axis=0)
    before = jnp.concatenate([jnp.ones_like(passing[:1]), through[:-1]], axis=0)
    colour = jnp.sum(before[None] * emitted, axis=1)
    return jnp.concatenate([colour, (1.0 - through[-1])[None]], axis=0)


def over_image(nearer, farther):
    return nearer + (1.0 - nearer[3:4]) * farther


def propagate(light_front, transmit):

    def advance(carried, factor):
        return (blur_columns(carried * factor), None)

    result, _ = lax.scan(advance, light_front, transmit)
    return result


def body(density, occupied, view_sign, transfer, absorb, light_in):
    cells_x, cells_y, columns = density.shape
    light_count = lax.axis_size("light")
    view_count = lax.axis_size("view")
    total_x = cells_x * light_count
    total_y = cells_y * view_count
    light_pos = lax.axis_index("light")
    view_pos = lax.axis_index("view")
    facing_back = (view_sign[0] < 0.0).astype(jnp.int32)
    path_length = 2.0 / total_y / jnp.abs(view_sign[0])
    padded = with_halo(density, (("light", 0),), 1).astype(jnp.float32)
    centre = padded[1:-1, :, :]
    grad_x = 0.5 * (padded[2:, :, :] - padded[:-2, :, :])
    side_y = jnp.pad(centre, ((0, 0), (1, 1), (0, 0)), mode="edge")
    grad_y = 0.5 * (side_y[:, 2:, :] - side_y[:, :-2, :])
    side_z = jnp.pad(centre, ((0, 0), (0, 0), (1, 1)))
    grad_z = 0.5 * (side_z[:, :, 2:] - side_z[:, :, :-2])
    bricks = occupied.shape[2]
    occupancy = jnp.broadcast_to(
        occupied[0, 0].astype(jnp.float32)[:, None], (bricks, columns // bricks)
    ).reshape(columns)
    extinction = jax.nn.softplus(polynomial(transfer[0], centre)) * occupancy
    opacity = 1.0 - jnp.exp(-extinction * path_length)
    colour = jnp.stack(
        [jax.nn.sigmoid(polynomial(transfer[channel], centre)) for channel in (1, 2, 3)], axis=1
    )
    facing = (0.8 * grad_x + 0.36 * grad_y + 0.48 * grad_z) * lax.rsqrt(
        1.0 + grad_x * grad_x + grad_y * grad_y + grad_z * grad_z
    )
    shading = 0.65 + 0.35 * facing
    transmit = jnp.exp(-absorb[None, :, None, None] * extinction[:, None] / total_x)
    incoming = light_in
    for turn_index in range(light_count - 1):
        outgoing = propagate(incoming, transmit)
        arrived = from_behind(outgoing.astype(jnp.bfloat16), "light", 1).astype(outgoing.dtype)
        incoming = jnp.where(light_pos == 0, light_in, arrived)

    def shade_layer(light_front, layer):
        layer_opacity, layer_colour, layer_shading, layer_transmit = layer
        emitted = layer_opacity[None] * layer_colour * (0.2 + light_front * layer_shading[None])
        pixel_row = composite_depth(emitted, layer_opacity, facing_back)
        return (blur_columns(light_front * layer_transmit), pixel_row)

    _, pixel_rows = lax.scan(shade_layer, incoming, (opacity, colour, shading, transmit))
    partial_image = jnp.transpose(pixel_rows, (1, 0, 2)).reshape(4, cells_x * columns)
    piece_len = cells_x * columns // view_count
    held = partial_image.reshape(4, view_count, piece_len)
    rounds = view_count.bit_length() - 1
    for level_bit in range(rounds):
        paired = held.reshape(4, held.shape[1] // 2, 2, piece_len)
        my_bit = jnp.bitwise_and(jnp.right_shift(view_pos, level_bit), 1)
        lower_half = paired[:, :, 0, :]
        upper_half = paired[:, :, 1, :]
        retained = jnp.where(my_bit == 0, lower_half, upper_half)
        outbound = jnp.where(my_bit == 0, upper_half, lower_half)
        received = from_partner(outbound, "view", level_bit)
        in_front = my_bit == facing_back
        nearer = jnp.where(in_front, retained, received)
        farther = jnp.where(in_front, received, retained)
        held = over_image(nearer, farther)
    return held.reshape(4, piece_len)


def solution(mesh):
    in_specs = (
        P("light", "view", None),
        P("light", "view", None),
        P(),
        P(),
        P(),
        P(None, "view", None),
    )
    out_specs = P(None, ("light", "view"))
    return jax.shard_map(body, mesh=mesh, in_specs=in_specs, out_specs=out_specs, check_vma=False)
```

profile of v0, /device:TPU:30, one launch (start us, length us, event | category | flops | bytes accessed | tf_op | source)
XLA Modules:
  0.0 154.8 jit_solution(9657700583977450405)
XLA Ops:
  0.9 4.7 %collective-permute-start = (bf16[1,16,2048]{2,1,0:T(8,128)(2,1)S(1)}, bf16[1,16,2048]{2,1,0:T(8,128)(2,1)S(1)}, u32[]{:S(2)}, u32[]{:S(2)}) collective-permute-start(bf16[1,16,2048]{2,1,0:T(8,128)(2,1)S(1)} %get-tuple-element.490), channel_id=1, source_target_pairs={{0,64},{64,128},{128,192},{192,256},{256,320},{320,384},{384,448},... | collective-permute-start | bytes 196616 | tf_op jit(solution)/shard_map/ppermute | solution.py:15
  5.6 1.9 %collective-permute-start.1 = (bf16[1,16,2048]{2,1,0:T(8,128)(2,1)S(1)}, bf16[1,16,2048]{2,1,0:T(8,128)(2,1)S(1)}, u32[]{:S(2)}, u32[]{:S(2)}) collective-permute-start(bf16[1,16,2048]{2,1,0:T(8,128)(2,1)S(1)} %get-tuple-element.491), channel_id=1, source_target_pairs={{64,0},{128,64},{192,128},{256,192},{320,256},{384,320},{448,384},... | collective-permute-start | bytes 196616 | tf_op jit(solution)/shard_map/ppermute | solution.py:17
  9.6 2.0 %fusion.64 = (f32[1,1]{1,0:T(1,128)}, f32[1,1]{1,0:T(1,128)}, f32[1,1]{1,0:T(1,128)}, f32[1,1]{1,0:T(1,128)}, f32[1,1]{1,0:T(1,128)}, /*index=5*/f32[1,1]{1,0:T(...) fusion(f32[4,4]{1,0:T(4,128)} %param.25), kind=kLoop, calls=%fused_computation.149 | loop fusion | bytes 128 | tf_op jit(solution)/shard_map/slice | solution.py:37
  11.6 1.4 collective-permute-done.1
  13.0 1.0 maximum_convert_fusion
  14.0 6.7 %exponential_subtract_fusion = (f32[4,16,2048]{2,1,0:T(8,128)}, f32[4,16,2048]{2,1,0:T(8,128)S(1)}, f32[4,16,2048]{2,1,0:T(8,128)}, f32[4,1,16,2048]{3,2,0,1:T(8,128)}) fusion(f32[]{:T(128)} %bitcast.19, f32[2048]{0:T(1024)S(1)} %broadcast_bitcast_fusion, f32[]{:T(128)} %bitcast.16, f32[]{:T(128)} %bitcast.15, f32[]{:T(128)} %bitcast.14, ...), kind=kLoop, calls=%fused_computation.80 | loop fusion | flops 3276800 | bytes 2629668 | tf_op jit(solution)/shard_map/sub | solution.py:91
  21.7 1.3 while.98
  23.7 3.8 %collective-permute-start.2 = (bf16[3,16,2048]{2,1,0:T(8,128)(2,1)}, bf16[3,16,2048]{2,1,0:T(8,128)(2,1)S(1)}, u32[]{:S(2)}, u32[]{:S(2)}) collective-permute-start(bf16[3,16,2048]{2,1,0:T(8,128)(2,1)} %convert_element_type.93), channel_id=1, source_target_pairs={{0,64},{64,128},{128,192},{192,256},{256,320},{320,384},{384,448},... | collective-permute-start | bytes 589832 | tf_op jit(solution)/shard_map/ppermute | solution.py:27
  27.5 4.0 %collective-permute-done.2 = bf16[3,16,2048]{2,1,0:T(8,128)(2,1)S(1)} collective-permute-done((bf16[3,16,2048]{2,1,0:T(8,128)(2,1)}, bf16[3,16,2048]{2,1,0:T(8,128)(2,1)S(1)}, u32[]{:S(2)}, u32[]{:S(2)}) %collective-permute-start.2) | collective-permute-done | bytes 196640 | tf_op jit(solution)/shard_map/ppermute | solution.py:27
  31.5 1.4 while.99
  33.6 5.4 %collective-permute-start.3 = (bf16[3,16,2048]{2,1,0:T(8,128)(2,1)}, bf16[3,16,2048]{2,1,0:T(8,128)(2,1)S(1)}, u32[]{:S(2)}, u32[]{:S(2)}) collective-permute-start(bf16[3,16,2048]{2,1,0:T(8,128)(2,1)} %convert_element_type.95), channel_id=1, source_target_pairs={{0,64},{64,128},{128,192},{192,256},{256,320},{320,384},{384,448},... | collective-permute-start | bytes 589832 | tf_op jit(solution)/shard_map/ppermute | solution.py:27
  39.0 3.5 %collective-permute-done.3 = bf16[3,16,2048]{2,1,0:T(8,128)(2,1)S(1)} collective-permute-done((bf16[3,16,2048]{2,1,0:T(8,128)(2,1)}, bf16[3,16,2048]{2,1,0:T(8,128)(2,1)S(1)}, u32[]{:S(2)}, u32[]{:S(2)}) %collective-permute-start.3) | collective-permute-done | bytes 196640 | tf_op jit(solution)/shard_map/ppermute | solution.py:27
  42.5 1.4 while.100
  44.6 5.5 %collective-permute-start.4 = (bf16[3,16,2048]{2,1,0:T(8,128)(2,1)}, bf16[3,16,2048]{2,1,0:T(8,128)(2,1)S(1)}, u32[]{:S(2)}, u32[]{:S(2)}) collective-permute-start(bf16[3,16,2048]{2,1,0:T(8,128)(2,1)} %convert_element_type.97), channel_id=1, source_target_pairs={{0,64},{64,128},{128,192},{192,256},{256,320},{320,384},{384,448},... | collective-permute-start | bytes 589832 | tf_op jit(solution)/shard_map/ppermute | solution.py:27
  50.1 3.5 %collective-permute-done.4 = bf16[3,16,2048]{2,1,0:T(8,128)(2,1)S(1)} collective-permute-done((bf16[3,16,2048]{2,1,0:T(8,128)(2,1)}, bf16[3,16,2048]{2,1,0:T(8,128)(2,1)S(1)}, u32[]{:S(2)}, u32[]{:S(2)}) %collective-permute-start.4) | collective-permute-done | bytes 196640 | tf_op jit(solution)/shard_map/ppermute | solution.py:27
  53.6 1.4 while.101
  55.7 5.5 %collective-permute-start.5 = (bf16[3,16,2048]{2,1,0:T(8,128)(2,1)}, bf16[3,16,2048]{2,1,0:T(8,128)(2,1)S(1)}, u32[]{:S(2)}, u32[]{:S(2)}) collective-permute-start(bf16[3,16,2048]{2,1,0:T(8,128)(2,1)} %convert_element_type.99), channel_id=1, source_target_pairs={{0,64},{64,128},{128,192},{192,256},{256,320},{320,384},{384,448},... | collective-permute-start | bytes 589832 | tf_op jit(solution)/shard_map/ppermute | solution.py:27
  61.2 3.5 %collective-permute-done.5 = bf16[3,16,2048]{2,1,0:T(8,128)(2,1)S(1)} collective-permute-done((bf16[3,16,2048]{2,1,0:T(8,128)(2,1)}, bf16[3,16,2048]{2,1,0:T(8,128)(2,1)S(1)}, u32[]{:S(2)}, u32[]{:S(2)}) %collective-permute-start.5) | collective-permute-done | bytes 196640 | tf_op jit(solution)/shard_map/ppermute | solution.py:27
  64.7 1.4 while.102
  66.1 5.5 %collective-permute-start.6 = (bf16[3,16,2048]{2,1,0:T(8,128)(2,1)S(1)}, bf16[3,16,2048]{2,1,0:T(8,128)(2,1)S(1)}, u32[]{:S(2)}, u32[]{:S(2)}) collective-permute-start(bf16[3,16,2048]{2,1,0:T(8,128)(2,1)S(1)} %convert_element_type.101), channel_id=1, source_target_pairs={{0,64},{64,128},{128,192},{192,256},{256,320},{320,384},{384,448},... | collective-permute-start | bytes 589832 | tf_op jit(solution)/shard_map/ppermute | solution.py:27
  72.3 2.5 %collective-permute-done.6 = bf16[3,16,2048]{2,1,0:T(8,128)(2,1)S(1)} collective-permute-done((bf16[3,16,2048]{2,1,0:T(8,128)(2,1)S(1)}, bf16[3,16,2048]{2,1,0:T(8,128)(2,1)S(1)}, u32[]{:S(2)}, u32[]{:S(2)}) %collective-permute-start.6) | collective-permute-done | bytes 196640 | tf_op jit(solution)/shard_map/ppermute | solution.py:27
  74.9 1.4 while.103
  76.3 5.6 %collective-permute-start.7 = (bf16[3,16,2048]{2,1,0:T(8,128)(2,1)S(1)}, bf16[3,16,2048]{2,1,0:T(8,128)(2,1)S(1)}, u32[]{:S(2)}, u32[]{:S(2)}) collective-permute-start(bf16[3,16,2048]{2,1,0:T(8,128)(2,1)S(1)} %convert_element_type.103), channel_id=1, source_target_pairs={{0,64},{64,128},{128,192},{192,256},{256,320},{320,384},{384,448},... | collective-permute-start | bytes 589832 | tf_op jit(solution)/shard_map/ppermute | solution.py:27
  81.9 8.6 %multiply_add_fusion = (f32[4,16,2048]{2,1,0:T(8,128)}, f32[4,1,16,2048]{3,2,0,1:T(8,128)}, f32[4,1,16,2048]{3,2,0,1:T(8,128)}) fusion(f32[4,16,2048]{2,1,0:T(8,128)} %get-tuple-element.486, f32[4,1,2048]{2,1,0:T(1,128)S(1)} %copy-done.6, f32[4,1,2048]{2,1,0:T(1,128)S(1)} %copy-done.5, f32[6,16,2048]{2,1,0:T(8,128)S(1)} %maximum_convert_fusion, f32[]{:T(128)} %bitcast.23, ...), kind=kLoop, calls=%fused_computation.76 | loop fusion | flops 5242880 | bytes 3735584 | tf_op jit(solution)/shard_map/add | solution.py:98
  90.5 1.4 while.104
  91.9 1.9 %collective-permute-start.8 = (bf16[3,16,2048]{2,1,0:T(8,128)(2,1)S(1)}, bf16[3,16,2048]{2,1,0:T(8,128)(2,1)S(1)}, u32[]{:S(2)}, u32[]{:S(2)}) collective-permute-start(bf16[3,16,2048]{2,1,0:T(8,128)(2,1)S(1)} %convert_element_type.105), channel_id=1, source_target_pairs={{0,64},{64,128},{128,192},{192,256},{256,320},{320,384},{384,448},... | collective-permute-start | bytes 589832 | tf_op jit(solution)/shard_map/ppermute | solution.py:27
  93.9 2.4 %pad_maximum_fusion = f32[4,3,16,2048]{3,2,0,1:T(8,128)} fusion(f32[4,1,16,2048]{3,2,0,1:T(8,128)} %get-tuple-element.485, f32[4,1,16,2048]{3,2,0,1:T(8,128)S(1)} %copy-done.2, f32[4,1,16,2048]{3,2,0,1:T(8,128)S(1)} %copy-done.3), kind=kLoop, calls=%fused_computation.65 | loop fusion | flops 786432 | bytes 3145728 | tf_op jit(solution)/shard_map/stack | solution.py:92
  96.3 3.2 %collective-permute-done.8 = bf16[3,16,2048]{2,1,0:T(8,128)(2,1)S(1)} collective-permute-done((bf16[3,16,2048]{2,1,0:T(8,128)(2,1)S(1)}, bf16[3,16,2048]{2,1,0:T(8,128)(2,1)S(1)}, u32[]{:S(2)}, u32[]{:S(2)}) %collective-permute-start.8) | collective-permute-done | bytes 196640 | tf_op jit(solution)/shard_map/ppermute | solution.py:27
  99.5 13.4 %while.105 = (s32[]{:T(128)}, f32[3,16,2048]{2,1,0:T(8,128)S(1)}, f32[4,4,2048]{2,1,0:T(4,128)S(1)}, f32[4,3,16,2048]{3,2,1,0:T(8,128)S(1)}, pred[]{:T(512)}, /*...) while((s32[]{:T(128)}, f32[3,16,2048]{2,1,0:T(8,128)S(1)}, ...), condition=%wide.region_17.18_spmd, body=%wide.region_14.17_spmd.sunk | while | flops 1839106 | bytes 6529147 | solution.py:112
  99.6 1.0 dynamic-slice_bitcast_fusion.3
  100.6 1.1 fusion.82
  102.9 1.0 dynamic-slice_bitcast_fusion.3
  103.9 1.1 fusion.82
  107.2 1.1 fusion.82
  109.6 1.0 dynamic-slice_bitcast_fusion.3
  110.6 1.1 fusion.82
  113.3 1.9 %collective-permute-start.9 = (f32[4,32,128]{2,1,0:T(8,128)S(1)}, f32[4,32,128]{2,1,0:T(8,128)S(1)}, u32[]{:S(2)}, u32[]{:S(2)}) collective-permute-start(f32[4,32,128]{2,1,0:T(8,128)S(1)} %bitcast.210), channel_id=1, source_target_pairs={{0,1},{1,0},{2,3},{3,2},{4,5},{5,4},{6,7},{7,6},{8,9},{9,8},{10,11... | collective-permute-start | bytes 196616 | tf_op jit(solution)/shard_map/ppermute | solution.py:33
  115.2 1.2 collective-permute-done.9
  116.6 2.7 %collective-permute-start.10 = (f32[4,16,128]{2,1,0:T(8,128)S(1)}, f32[4,16,128]{2,1,0:T(8,128)S(1)}, u32[]{:S(2)}, u32[]{:S(2)}) collective-permute-start(f32[4,16,128]{2,1,0:T(8,128)S(1)} %bitcast.216), channel_id=1, source_target_pairs={{0,2},{1,3},{2,0},{3,1},{4,6},{5,7},{6,4},{7,5},{8,10},{9,11},{10,... | collective-permute-start | bytes 98312 | tf_op jit(solution)/shard_map/ppermute | solution.py:33
  119.3 3.1 %collective-permute-done.10 = f32[4,16,128]{2,1,0:T(8,128)S(1)} collective-permute-done((f32[4,16,128]{2,1,0:T(8,128)S(1)}, f32[4,16,128]{2,1,0:T(8,128)S(1)}, u32[]{:S(2)}, u32[]{:S(2)}) %collective-permute-start.10) | collective-permute-done | bytes 32800 | tf_op jit(solution)/shard_map/ppermute | solution.py:33
  122.5 3.3 %collective-permute-start.11 = (f32[4,8,128]{2,1,0:T(8,128)S(1)}, f32[4,8,128]{2,1,0:T(8,128)S(1)}, u32[]{:S(2)}, u32[]{:S(2)}) collective-permute-start(f32[4,8,128]{2,1,0:T(8,128)S(1)} %bitcast.222), channel_id=1, source_target_pairs={{0,4},{1,5},{2,6},{3,7},{4,0},{5,1},{6,2},{7,3},{8,12},{9,13},{10,... | collective-permute-start | bytes 49160 | tf_op jit(solution)/shard_map/ppermute | solution.py:33
  125.8 3.8 %collective-permute-done.11 = f32[4,8,128]{2,1,0:T(8,128)S(1)} collective-permute-done((f32[4,8,128]{2,1,0:T(8,128)S(1)}, f32[4,8,128]{2,1,0:T(8,128)S(1)}, u32[]{:S(2)}, u32[]{:S(2)}) %collective-permute-start.11) | collective-permute-done | bytes 16416 | tf_op jit(solution)/shard_map/ppermute | solution.py:33
  129.6 4.3 %collective-permute-start.12 = (f32[4,4,128]{2,1,0:T(4,128)S(1)}, f32[4,4,128]{2,1,0:T(4,128)S(1)}, u32[]{:S(2)}, u32[]{:S(2)}) collective-permute-start(f32[4,4,128]{2,1,0:T(4,128)S(1)} %bitcast.223), channel_id=1, source_target_pairs={{0,8},{1,9},{2,10},{3,11},{4,12},{5,13},{6,14},{7,15},{8,0},{9,1},... | collective-permute-start | bytes 24584 | tf_op jit(solution)/shard_map/ppermute | solution.py:33
  133.9 1.6 %collective-permute-done.12 = f32[4,4,128]{2,1,0:T(4,128)S(1)} collective-permute-done((f32[4,4,128]{2,1,0:T(4,128)S(1)}, f32[4,4,128]{2,1,0:T(4,128)S(1)}, u32[]{:S(2)}, u32[]{:S(2)}) %collective-permute-start.12) | collective-permute-done | bytes 8224 | tf_op jit(solution)/shard_map/ppermute | solution.py:33
  135.6 6.1 %collective-permute-start.13 = (f32[4,2,128]{2,1,0:T(2,128)S(1)}, f32[4,2,128]{2,1,0:T(2,128)S(1)}, u32[]{:S(2)}, u32[]{:S(2)}) collective-permute-start(f32[4,2,128]{2,1,0:T(2,128)S(1)} %bitcast.224), channel_id=1, source_target_pairs={{0,16},{1,17},{2,18},{3,19},{4,20},{5,21},{6,22},{7,23},{8,24},{9,... | collective-permute-start | bytes 12296 | tf_op jit(solution)/shard_map/ppermute | solution.py:33
  141.7 1.6 %collective-permute-done.13 = f32[4,2,128]{2,1,0:T(2,128)S(1)} collective-permute-done((f32[4,2,128]{2,1,0:T(2,128)S(1)}, f32[4,2,128]{2,1,0:T(2,128)S(1)}, u32[]{:S(2)}, u32[]{:S(2)}) %collective-permute-start.13) | collective-permute-done | bytes 4128 | tf_op jit(solution)/shard_map/ppermute | solution.py:33
  143.3 9.3 %collective-permute-start.14 = (f32[4,1,128]{2,0,1:T(4,128)S(1)}, f32[4,1,128]{2,0,1:T(4,128)S(1)}, u32[]{:S(2)}, u32[]{:S(2)}) collective-permute-start(f32[4,1,128]{2,0,1:T(4,128)S(1)} %bitcast.225), channel_id=1, source_target_pairs={{0,32},{1,33},{2,34},{3,35},{4,36},{5,37},{6,38},{7,39},{8,40},{9,... | collective-permute-start | bytes 6152 | tf_op jit(solution)/shard_map/ppermute | solution.py:33
  152.6 1.5 collective-permute-done.14
  (158 shorter events, 22.9 us)
Async XLA Ops:
  0.9 10.7 %collective-permute-start = (bf16[1,16,2048]{2,1,0:T(8,128)(2,1)S(1)}, bf16[1,16,2048]{2,1,0:T(8,128)(2,1)S(1)}, u32[]{:S(2)}, u32[]{:S(2)}) collective-permute-start(bf16[1,16,2048]{2,1,0:T(8,128)(2,1)S(1)} %get-tuple-element.490), channel_id=1, source_target_pairs={{0,64},{64,128},{128,192},{192,256},{256,320},{320,384},{384,448},... | collective-permute-start | bytes 196616 | tf_op jit(solution)/shard_map/ppermute | solution.py:15
  5.6 7.4 %collective-permute-start.1 = (bf16[1,16,2048]{2,1,0:T(8,128)(2,1)S(1)}, bf16[1,16,2048]{2,1,0:T(8,128)(2,1)S(1)}, u32[]{:S(2)}, u32[]{:S(2)}) collective-permute-start(bf16[1,16,2048]{2,1,0:T(8,128)(2,1)S(1)} %get-tuple-element.491), channel_id=1, source_target_pairs={{64,0},{128,64},{192,128},{256,192},{320,256},{384,320},{448,384},... | collective-permute-start | bytes 196616 | tf_op jit(solution)/shard_map/ppermute | solution.py:17
  20.7 1.0 copy-start.1
  21.7 9.8 %copy-start = (f32[3,16,2048]{2,1,0:T(8,128)S(1)}, f32[3,16,2048]{2,1,0:T(8,128)}, u32[]{:S(2)}) copy-start(f32[3,16,2048]{2,1,0:T(8,128)} %param.27) | copy-start | bytes 1179652
  23.7 7.8 %collective-permute-start.2 = (bf16[3,16,2048]{2,1,0:T(8,128)(2,1)}, bf16[3,16,2048]{2,1,0:T(8,128)(2,1)S(1)}, u32[]{:S(2)}, u32[]{:S(2)}) collective-permute-start(bf16[3,16,2048]{2,1,0:T(8,128)(2,1)} %convert_element_type.93), channel_id=1, source_target_pairs={{0,64},{64,128},{128,192},{192,256},{256,320},{320,384},{384,448},... | collective-permute-start | bytes 589832 | tf_op jit(solution)/shard_map/ppermute | solution.py:27
  33.6 8.9 %collective-permute-start.3 = (bf16[3,16,2048]{2,1,0:T(8,128)(2,1)}, bf16[3,16,2048]{2,1,0:T(8,128)(2,1)S(1)}, u32[]{:S(2)}, u32[]{:S(2)}) collective-permute-start(bf16[3,16,2048]{2,1,0:T(8,128)(2,1)} %convert_element_type.95), channel_id=1, source_target_pairs={{0,64},{64,128},{128,192},{192,256},{256,320},{320,384},{384,448},... | collective-permute-start | bytes 589832 | tf_op jit(solution)/shard_map/ppermute | solution.py:27
  44.6 9.0 %collective-permute-start.4 = (bf16[3,16,2048]{2,1,0:T(8,128)(2,1)}, bf16[3,16,2048]{2,1,0:T(8,128)(2,1)S(1)}, u32[]{:S(2)}, u32[]{:S(2)}) collective-permute-start(bf16[3,16,2048]{2,1,0:T(8,128)(2,1)} %convert_element_type.97), channel_id=1, source_target_pairs={{0,64},{64,128},{128,192},{192,256},{256,320},{320,384},{384,448},... | collective-permute-start | bytes 589832 | tf_op jit(solution)/shard_map/ppermute | solution.py:27
  55.7 9.0 %collective-permute-start.5 = (bf16[3,16,2048]{2,1,0:T(8,128)(2,1)}, bf16[3,16,2048]{2,1,0:T(8,128)(2,1)S(1)}, u32[]{:S(2)}, u32[]{:S(2)}) collective-permute-start(bf16[3,16,2048]{2,1,0:T(8,128)(2,1)} %convert_element_type.99), channel_id=1, source_target_pairs={{0,64},{64,128},{128,192},{192,256},{256,320},{320,384},{384,448},... | collective-permute-start | bytes 589832 | tf_op jit(solution)/shard_map/ppermute | solution.py:27
  64.7 6.9 %copy-start.4 = (bf16[4,16,2048]{2,1,0:T(8,128)(2,1)S(1)}, bf16[4,16,2048]{2,1,0:T(8,128)(2,1)}, u32[]{:S(2)}) copy-start(bf16[4,16,2048]{2,1,0:T(8,128)(2,1)} %param.22) | copy-start | bytes 786436
  66.1 8.7 %collective-permute-start.6 = (bf16[3,16,2048]{2,1,0:T(8,128)(2,1)S(1)}, bf16[3,16,2048]{2,1,0:T(8,128)(2,1)S(1)}, u32[]{:S(2)}, u32[]{:S(2)}) collective-permute-start(bf16[3,16,2048]{2,1,0:T(8,128)(2,1)S(1)} %convert_element_type.101), channel_id=1, source_target_pairs={{0,64},{64,128},{128,192},{192,256},{256,320},{320,384},{384,448},... | collective-permute-start | bytes 589832 | tf_op jit(solution)/shard_map/ppermute | solution.py:27
  74.8 7.0 %copy-start.5 = (f32[4,1,2048]{2,1,0:T(1,128)S(1)}, f32[4,1,2048]{2,1,0:T(1,128)}, u32[]{:S(2)}) copy-start(f32[4,1,2048]{2,1,0:T(1,128)} %get-tuple-element.488) | copy-start | bytes 98308
  74.8 7.0 %copy-start.6 = (f32[4,1,2048]{2,1,0:T(1,128)S(1)}, f32[4,1,2048]{2,1,0:T(1,128)}, u32[]{:S(2)}) copy-start(f32[4,1,2048]{2,1,0:T(1,128)} %get-tuple-element.489) | copy-start | bytes 98308
  76.3 14.2 %collective-permute-start.7 = (bf16[3,16,2048]{2,1,0:T(8,128)(2,1)S(1)}, bf16[3,16,2048]{2,1,0:T(8,128)(2,1)S(1)}, u32[]{:S(2)}, u32[]{:S(2)}) collective-permute-start(bf16[3,16,2048]{2,1,0:T(8,128)(2,1)S(1)} %convert_element_type.103), channel_id=1, source_target_pairs={{0,64},{64,128},{128,192},{192,256},{256,320},{320,384},{384,448},... | collective-permute-start | bytes 589832 | tf_op jit(solution)/shard_map/ppermute | solution.py:27
  90.5 3.4 %copy-start.2 = (f32[4,1,16,2048]{3,2,0,1:T(8,128)S(1)}, f32[4,1,16,2048]{3,2,0,1:T(8,128)}, u32[]{:S(2)}) copy-start(f32[4,1,16,2048]{3,2,0,1:T(8,128)} %get-tuple-element.487) | copy-start | bytes 1572868
  90.5 3.4 %copy-start.3 = (f32[4,1,16,2048]{3,2,0,1:T(8,128)S(1)}, f32[4,1,16,2048]{3,2,0,1:T(8,128)}, u32[]{:S(2)}) copy-start(f32[4,1,16,2048]{3,2,0,1:T(8,128)} %get-tuple-element.484) | copy-start | bytes 1572868
  91.9 7.6 %collective-permute-start.8 = (bf16[3,16,2048]{2,1,0:T(8,128)(2,1)S(1)}, bf16[3,16,2048]{2,1,0:T(8,128)(2,1)S(1)}, u32[]{:S(2)}, u32[]{:S(2)}) collective-permute-start(bf16[3,16,2048]{2,1,0:T(8,128)(2,1)S(1)} %convert_element_type.105), channel_id=1, source_target_pairs={{0,64},{64,128},{128,192},{192,256},{256,320},{320,384},{384,448},... | collective-permute-start | bytes 589832 | tf_op jit(solution)/shard_map/ppermute | solution.py:27
  93.9 5.7 %copy-start.7 = (f32[4,4,2048]{2,1,0:T(4,128)S(1)}, f32[4,4,2048]{2,1,0:T(4,128)}, u32[]{:S(2)}) copy-start(f32[4,4,2048]{2,1,0:T(4,128)} %custom-call) | copy-start | bytes 393220
  113.3 3.1 %collective-permute-start.9 = (f32[4,32,128]{2,1,0:T(8,128)S(1)}, f32[4,32,128]{2,1,0:T(8,128)S(1)}, u32[]{:S(2)}, u32[]{:S(2)}) collective-permute-start(f32[4,32,128]{2,1,0:T(8,128)S(1)} %bitcast.210), channel_id=1, source_target_pairs={{0,1},{1,0},{2,3},{3,2},{4,5},{5,4},{6,7},{7,6},{8,9},{9,8},{10,11... | collective-permute-start | bytes 196616 | tf_op jit(solution)/shard_map/ppermute | solution.py:33
  116.6 5.8 %collective-permute-start.10 = (f32[4,16,128]{2,1,0:T(8,128)S(1)}, f32[4,16,128]{2,1,0:T(8,128)S(1)}, u32[]{:S(2)}, u32[]{:S(2)}) collective-permute-start(f32[4,16,128]{2,1,0:T(8,128)S(1)} %bitcast.216), channel_id=1, source_target_pairs={{0,2},{1,3},{2,0},{3,1},{4,6},{5,7},{6,4},{7,5},{8,10},{9,11},{10,... | collective-permute-start | bytes 98312 | tf_op jit(solution)/shard_map/ppermute | solution.py:33
  122.5 7.1 %collective-permute-start.11 = (f32[4,8,128]{2,1,0:T(8,128)S(1)}, f32[4,8,128]{2,1,0:T(8,128)S(1)}, u32[]{:S(2)}, u32[]{:S(2)}) collective-permute-start(f32[4,8,128]{2,1,0:T(8,128)S(1)} %bitcast.222), channel_id=1, source_target_pairs={{0,4},{1,5},{2,6},{3,7},{4,0},{5,1},{6,2},{7,3},{8,12},{9,13},{10,... | collective-permute-start | bytes 49160 | tf_op jit(solution)/shard_map/ppermute | solution.py:33
  129.6 5.9 %collective-permute-start.12 = (f32[4,4,128]{2,1,0:T(4,128)S(1)}, f32[4,4,128]{2,1,0:T(4,128)S(1)}, u32[]{:S(2)}, u32[]{:S(2)}) collective-permute-start(f32[4,4,128]{2,1,0:T(4,128)S(1)} %bitcast.223), channel_id=1, source_target_pairs={{0,8},{1,9},{2,10},{3,11},{4,12},{5,13},{6,14},{7,15},{8,0},{9,1},... | collective-permute-start | bytes 24584 | tf_op jit(solution)/shard_map/ppermute | solution.py:33
  135.6 7.7 %collective-permute-start.13 = (f32[4,2,128]{2,1,0:T(2,128)S(1)}, f32[4,2,128]{2,1,0:T(2,128)S(1)}, u32[]{:S(2)}, u32[]{:S(2)}) collective-permute-start(f32[4,2,128]{2,1,0:T(2,128)S(1)} %bitcast.224), channel_id=1, source_target_pairs={{0,16},{1,17},{2,18},{3,19},{4,20},{5,21},{6,22},{7,23},{8,24},{9,... | collective-permute-start | bytes 12296 | tf_op jit(solution)/shard_map/ppermute | solution.py:33
  143.3 10.8 %collective-permute-start.14 = (f32[4,1,128]{2,0,1:T(4,128)S(1)}, f32[4,1,128]{2,0,1:T(4,128)S(1)}, u32[]{:S(2)}, u32[]{:S(2)}) collective-permute-start(f32[4,1,128]{2,0,1:T(4,128)S(1)} %bitcast.225), channel_id=1, source_target_pairs={{0,32},{1,33},{2,34},{3,35},{4,36},{5,37},{6,38},{7,39},{8,40},{9,... | collective-permute-start | bytes 6152 | tf_op jit(solution)/shard_map/ppermute | solution.py:33
where the time goes:
time: 156 us; the launch traced here: 155 us
  starting transfers between devices  67.4 us (43%)
  other arithmetic  40.5 us (26%)
  waiting for transfers between devices  34.2 us (22%)
  local copies, waits for them, and re-layouts  10.4 us (7%)
    ppermute x7, starting transfers between devices, from_behind(): return lax.ppermute(x, axis, pairs)  33.1 us
    ppermute x6, starting transfers between devices, from_partner(): return lax.ppermute(value, axis, pairs)  27.6 us
    ppermute x7, waiting for transfers between devices, from_behind(): return lax.ppermute(x, axis, pairs)  20.1 us
    ppermute x6, waiting for transfers between devices, from_partner(): return lax.ppermute(value, axis, pairs)  12.8 us
    add x32, other arithmetic, blur_columns(): 0.25 * padded[..., :-2] + 0.5 * padded[..., 1:-1] + 0.25 * padded[..., 2:]  8.64 us
    add x1, other arithmetic, body(): shading = 0.65 + 0.35 * facing  8.57 us
    sub x1, other arithmetic, body(): opacity = 1.0 - jnp.exp(-extinction * path_length)  6.68 us
    ppermute x1, starting transfers between devices, with_halo(): lax.ppermute(tail, axis, [(i, (i + 1) % count) for i in range(ends)])  4.7 us
  transfers between devices with their start and end apart: 15, of which 13 were waited for; matrix products, arithmetic and copies ran while one was open for 10% of the time, Pallas kernels for 0%

commit v1 on v0

v1 whole, which is shorter than its diff:
```python
import jax
import jax.numpy as jnp
from jax import lax
from jax.experimental import pallas as pl
from jax.experimental.pallas import tpu as pltpu
from jax.sharding import PartitionSpec as P

S = 8
T = 256
H = 128
F32 = jnp.float32
BF16 = jnp.bfloat16
VMEM = pl.BlockSpec(memory_space=pltpu.VMEM)
SMEM = pl.BlockSpec(memory_space=pltpu.SMEM)


def halves(x):
    return x[..., :H], x[..., H:]


def lane_is(pos):
    return lax.broadcasted_iota(jnp.int32, (S, H), 1) == pos


def sub_is(pos):
    return lax.broadcasted_iota(jnp.int32, (S, H), 0) == pos


def previous(a, b):
    ra, rb = pltpu.roll(a, 1, a.ndim - 1), pltpu.roll(b, 1, a.ndim - 1)
    wrap = jnp.where(sub_is(0), 0.0, pltpu.roll(rb, 1, a.ndim - 2))
    first = lane_is(0)
    return jnp.where(first, wrap, ra), jnp.where(first, ra, rb)


def following(a, b):
    ra, rb = pltpu.roll(a, H - 1, a.ndim - 1), pltpu.roll(b, H - 1, a.ndim - 1)
    wrap = jnp.where(sub_is(S - 1), 0.0, pltpu.roll(ra, S - 1, a.ndim - 2))
    last = lane_is(H - 1)
    return jnp.where(last, rb, ra), jnp.where(last, wrap, rb)


def blur(a, b):
    pa, pb = previous(a, b)
    na, nb = following(a, b)
    return 0.25 * (pa + na) + 0.5 * a, 0.25 * (pb + nb) + 0.5 * b


def polynomial(coeffs, row, s):
    return coeffs[row, 0] + s * (coeffs[row, 1] + s * (coeffs[row, 2] + s * coeffs[row, 3]))


def softplus(x):
    u = jnp.exp(-jnp.abs(x))
    tail = jnp.where(u < 2.0**-8, u * (1.0 - u * (0.5 - u * (1.0 / 3.0))), jnp.log(1.0 + u))
    return jnp.maximum(x, 0.0) + tail


def brick_mask(occ_ref):
    sub = lax.broadcasted_iota(jnp.int32, (S, H), 0)
    out = []
    for h in range(2):
        occ = jnp.zeros((S, H), F32)
        for s in range(S):
            occ = jnp.where(sub == s, occ_ref[0, 0, 2 * s + h].astype(F32), occ)
        out.append(occ)
    return out


def prepare_kernel(dens_ref, occ_ref, light_ref, pos_ref, cells_ref, first_ref, last_ref, send_ref, rows_ref, tmp):
    layers, rows, _ = dens_ref.shape
    occ = brick_mask(occ_ref)
    mask = jnp.concatenate(occ, axis=1)[None] > 0.5
    for layer in range(layers):
        x = dens_ref[layer].astype(F32)
        for s in range(S):
            for h in range(2):
                column = (2 * s + h) * H
                tmp[pl.ds(h * rows * S + s, rows, stride=S), :] = x[:, column : column + H]
        y = jnp.concatenate([tmp[h * rows * S : (h + 1) * rows * S, :].reshape(rows, S, H) for h in range(2)], axis=2)
        raw = y.astype(BF16)
        cells_ref[layer] = raw
        if layer == 0:
            first_ref[...] = raw
        if layer == layers - 1:
            last_ref[...] = raw
        masked = jnp.where(mask, y, -1.0).astype(BF16)
        send_ref[:, layer] = masked.reshape(rows // 2, 2, S, T)
    start = 2 * pos_ref[0]
    for c in range(3):
        for r in range(2):
            for s in range(S):
                rows_ref[c, r, s : s + 1, :] = light_ref[c, pl.ds(start + r, 1), s * T : (s + 1) * T]


def propagate_kernel(recv_ref, rows_ref, transfer_ref, absorb_ref, send_ref):
    blocks, layers = recv_ref.shape[0], recv_ref.shape[1]
    scale = [-absorb_ref[c] / 32.0 for c in range(3)]

    def block(k, carry):
        front = list(carry)
        for c in range(3):
            a, b = front[c]
            send_ref[k, c, :, :, :H] = a.astype(BF16)
            send_ref[k, c, :, :, H:] = b.astype(BF16)
        for layer in range(layers):
            ext = []
            for d in halves(recv_ref[k, layer].astype(F32)):
                ext.append(jnp.where(d < 0.0, 0.0, softplus(polynomial(transfer_ref, 0, d))))
            for c in range(3):
                a, b = front[c]
                front[c] = blur(a * jnp.exp(scale[c] * ext[0]), b * jnp.exp(scale[c] * ext[1]))
        return tuple(front)

    init = tuple(halves(rows_ref[c]) for c in range(3))
    final = lax.fori_loop(0, blocks - 1, block, init)
    for c in range(3):
        send_ref[blocks - 1, c, :, :, :H] = final[c][0].astype(BF16)
        send_ref[blocks - 1, c, :, :, H:] = final[c][1].astype(BF16)


def local_kernel(cells_ref, low_ref, high_ref, occ_ref, sign_ref, transfer_ref, ext_ref, gain_ref, base_ref, *, total_y):
    layers, rows = cells_ref.shape[0], cells_ref.shape[1]
    occ = brick_mask(occ_ref)
    sign = sign_ref[0]
    back = sign < 0.0
    path = (2.0 / total_y) / jnp.abs(jnp.full((S, H), sign, F32))

    def load(layer, r):
        if layer < 0:
            v = low_ref[r]
        elif layer >= layers:
            v = high_ref[r]
        else:
            v = cells_ref[layer, r]
        return halves(v.astype(F32))

    def row(i, carry):
        r = jnp.where(back, rows - 1 - i, i)
        up = jnp.minimum(r + 1, rows - 1)
        down = jnp.maximum(r - 1, 0)
        column = [load(layer, r) for layer in range(-1, layers + 1)]
        new = []
        for layer in range(layers):
            through, base = carry[layer]
            d = column[layer + 1]
            dn, dp = load(layer, up), load(layer, down)
            zp, zn = previous(*d), following(*d)
            t_out, b_out = [], []
            for h in range(2):
                s = d[h]
                gx = 0.5 * (column[layer + 2][h] - column[layer][h])
                gy = 0.5 * (dn[h] - dp[h])
                gz = 0.5 * (zn[h] - zp[h])
                facing = (0.8 * gx + 0.36 * gy + 0.48 * gz) * lax.rsqrt(1.0 + gx * gx + gy * gy + gz * gz)
                shading = 0.65 + 0.35 * facing
                ext = softplus(polynomial(transfer_ref, 0, s)) * occ[h]
                ext_ref[layer, r, :, h * H : (h + 1) * H] = ext
                passing = jnp.exp(-ext * path)
                weight = through[h] * (1.0 - passing)
                colours = []
                for c in range(3):
                    lit = weight * jax.nn.sigmoid(polynomial(transfer_ref, c + 1, s))
                    colours.append(base[h][c] + lit)
                    gain_ref[layer, r, c, :, h * H : (h + 1) * H] = lit * shading
                b_out.append(tuple(colours))
                t_out.append(through[h] * passing)
            new.append((tuple(t_out), tuple(b_out)))
        return tuple(new)

    one, zero = jnp.ones((S, H), F32), jnp.zeros((S, H), F32)
    init = tuple(((one, one), ((zero,) * 3, (zero,) * 3)) for _ in range(layers))
    final = lax.fori_loop(0, rows, row, init)
    for layer in range(layers):
        through, base = final[layer]
        for h in range(2):
            for c in range(3):
                base_ref[layer, c, :, h * H : (h + 1) * H] = 0.2 * base[h][c]
            base_ref[layer, 3, :, h * H : (h + 1) * H] = 1.0 - through[h]


def shade_kernel(front_ref, ext_ref, gain_ref, base_ref, absorb_ref, send_ref, tmp):
    layers, rows = ext_ref.shape[0], ext_ref.shape[1]
    scale = [-absorb_ref[c] / 32.0 for c in range(3)]

    def pair(i, carry):
        acc = [list(x) for x in carry]
        for q in range(2):
            r = 2 * i + q
            for c in range(3):
                a, b = halves(front_ref[i, c, q].astype(F32))
                for layer in range(layers):
                    ga, gb = halves(gain_ref[layer, r, c])
                    acc[layer][2 * c] += a * ga
                    acc[layer][2 * c + 1] += b * gb
                    if layer < layers - 1:
                        ea, eb = halves(ext_ref[layer, r])
                        a, b = blur(a * jnp.exp(scale[c] * ea), b * jnp.exp(scale[c] * eb))
        return tuple(tuple(x) for x in acc)

    init = tuple(
        tuple(base_ref[layer, c, :, h * H : (h + 1) * H] for c in range(3) for h in range(2))
        for layer in range(layers)
    )
    final = lax.fori_loop(0, rows // 2, pair, init)
    for layer in range(layers):
        for h in range(2):
            for c in range(4):
                if c < 3:
                    tmp[layer, c, h] = final[layer][2 * c + h]
                else:
                    tmp[layer, c, h] = base_ref[layer, 3, :, h * H : (h + 1) * H]
                for j in range(4):
                    send_ref[2 * j + h, c, 2 * layer : 2 * layer + 2, :] = tmp[layer, c, h, pl.ds(j, 2, stride=4), :]


def merge_kernel(parts_ref, sign_ref, send_ref):
    count = parts_ref.shape[0]
    back = sign_ref[0] < 0.0
    through, colour = None, None
    for i in range(count):
        k = jnp.where(back, count - 1 - i, i)
        part = [parts_ref[k, c] for c in range(4)]
        if colour is None:
            colour, through = part[:3], 1.0 - part[3]
        else:
            colour = [colour[c] + through * part[c] for c in range(3)]
            through = through * (1.0 - part[3])
    for c in range(3):
        send_ref[:, c, :] = colour[c]
    send_ref[:, 3, :] = 1.0 - through


def final_kernel(parts_ref, sign_ref, out_ref):
    count = parts_ref.shape[0]
    back = sign_ref[0] < 0.0
    held = None
    for i in range(count):
        k = jnp.where(back, count - 1 - i, i)
        part = parts_ref[k]
        held = part if held is None else held + (1.0 - held[3:4]) * part
    out_ref[...] = held


def body(density, occupied, view_sign, transfer, absorb, light_in):
    layers, rows, columns = density.shape
    lights = lax.axis_size("light")
    views = lax.axis_size("view")
    pos = lax.axis_index("light").astype(jnp.int32)[None]
    sds = jax.ShapeDtypeStruct

    cells, first, last, send, light_rows = pl.pallas_call(
        prepare_kernel,
        out_shape=(
            sds((layers, rows, S, T), BF16),
            sds((rows, S, T), BF16),
            sds((rows, S, T), BF16),
            sds((lights, layers, 2, S, T), BF16),
            sds((3, 2, S, T), F32),
        ),
        in_specs=[VMEM, SMEM, VMEM, SMEM],
        out_specs=(VMEM,) * 5,
        scratch_shapes=[pltpu.VMEM((2 * rows * S, H), F32)],
        name="prepare",
    )(density, occupied, light_in, pos)

    ends = lights - 1
    low = lax.ppermute(last, "light", [(i, i + 1) for i in range(ends)])
    high = lax.ppermute(first, "light", [(i + 1, i) for i in range(ends)])
    recv = lax.all_to_all(send, "light", 0, 0)

    ext, gain, base = pl.pallas_call(
        lambda *refs: local_kernel(*refs, total_y=rows * views),
        out_shape=(
            sds((layers, rows, S, T), F32),
            sds((layers, rows, 3, S, T), F32),
            sds((layers, 4, S, T), F32),
        ),
        in_specs=[VMEM, VMEM, VMEM, SMEM, SMEM, SMEM],
        out_specs=(VMEM,) * 3,
        name="local",
    )(cells, low, high, occupied, view_sign, transfer)

    fronts = pl.pallas_call(
        propagate_kernel,
        out_shape=sds((lights, 3, 2, S, T), BF16),
        in_specs=[VMEM, VMEM, SMEM, SMEM],
        out_specs=VMEM,
        name="propagate",
    )(recv, light_rows, transfer, absorb)
    front = lax.all_to_all(fronts, "light", 0, 0)

    partial = pl.pallas_call(
        shade_kernel,
        out_shape=sds((8, 4, 8, H), F32),
        in_specs=[VMEM, VMEM, VMEM, VMEM, SMEM],
        out_specs=VMEM,
        scratch_shapes=[pltpu.VMEM((layers, 4, 2, S, H), F32)],
        name="shade",
    )(front, ext, gain, base, absorb)

    near = [[z * 8 + k for k in range(8)] for z in range(views // 8)]
    far = [[z * 8 + k for z in range(views // 8)] for k in range(8)]
    parts = lax.all_to_all(partial, "view", 0, 0, axis_index_groups=near)
    merged = pl.pallas_call(
        merge_kernel,
        out_shape=sds((8, 4, H), F32),
        in_specs=[VMEM, SMEM],
        out_specs=VMEM,
        name="merge",
    )(parts, view_sign)
    parts = lax.all_to_all(merged, "view", 0, 0, axis_index_groups=far)
    return pl.pallas_call(
        final_kernel,
        out_shape=sds((4, H), F32),
        in_specs=[VMEM, SMEM],
        out_specs=VMEM,
        name="final",
    )(parts, view_sign)


def solution(mesh):
    in_specs = (
        P("light", "view", None),
        P("light", "view", None),
        P(),
        P(),
        P(),
        P(None, "view", None),
    )
    out_specs = P(None, ("light", "view"))
    return jax.shard_map(body, mesh=mesh, in_specs=in_specs, out_specs=out_specs, check_vma=False)
```

time: 156 us -> 83.9 us (0.54)
  the two profiles are of different devices: /device:TPU:30 before, /device:TPU:24 now
where the time goes in v1:
time: 83.9 us; the launch traced here: 83.2 us
  blocking collectives  44.7 us (53%)
  Pallas kernels  18.5 us (22%)
  starting transfers between devices  13.1 us (16%)
  waiting for transfers between devices  4.99 us (6%)
  local copies, waits for them, and re-layouts  1.29 us (2%)
    all_to_all x1, blocking collectives, body(): parts = lax.all_to_all(merged, 'view', 0, 0, axis_index_groups=far)  17.8 us
    all_to_all x1, blocking collectives, body(): recv = lax.all_to_all(send, 'light', 0, 0)  16.8 us
    all_to_all x1, blocking collectives, body(): parts = lax.all_to_all(partial, 'view', 0, 0, axis_index_groups=near)  10.1 us
    all_to_all x1, starting transfers between devices, body(): front = lax.all_to_all(fronts, 'light', 0, 0)  6.6 us
    ppermute x1, waiting for transfers between devices, body(): high = lax.ppermute(first, 'light', [(i + 1, i) for i in range(ends)])  4.98 us
    pallas_call x1, Pallas kernels, body(): pl.pallas_call(shade_kernel, out_shape=sds((8, 4, 8, H), F32), in_specs=[...  4.65 us
    ppermute x1, starting transfers between devices, body(): low = lax.ppermute(last, 'light', [(i, i + 1) for i in range(ends)])  4.58 us
    pallas_call x1, Pallas kernels, body(): pl.pallas_call(lambda *refs: local_kernel(*refs, total_y=rows * views), o...  4.51 us
  transfers between devices with their start and end apart: 3, of which 1 were waited for; matrix products, arithmetic and copies ran while one was open for 0% of the time, Pallas kernels for 5%

profile of v1, /device:TPU:24, one launch (start us, length us, event | category | flops | bytes accessed | tf_op | source)
XLA Modules:
  0.0 83.2 jit_solution(5142729224426261549)
XLA Ops:
  0.0 2.1 %prepare.1 = (bf16[4,16,8,256]{3,2,1,0:T(8,128)(2,1)}, bf16[16,8,256]{2,1,0:T(8,128)(2,1)}, bf16[16,8,256]{2,1,0:T(8,128)(2,1)}, bf16[8,4,2,8,256]{4,3,2,1,0:T(8,128)(2,1)}, f32[3,2,8,256]{3,2,1,0:T(8,128)}) custom-call(bf16[4,16,2048]{2,1,0:T(8,128)(2,1)} %dens_ref.1, s32[1,1,16]{2,1,0:T(1,128)} %refs_3_.1, f32[3,16,2048]{2,1,0:T(8,128)} %light_ref.1, ...), custom_call_target="tpu_custom_call" | custom-call | tf_op jit(solution)/shard_map/prepare/pallas_call | solution.py:252
  2.1 16.8 %all_to_all.20.recv_ref = bf16[8,4,2,8,256]{4,3,2,1,0:T(8,128)(2,1)} all-to-all(bf16[8,4,2,8,256]{4,3,2,1,0:T(8,128)(2,1)} %get-tuple-element.13), channel_id=1, replica_groups=mesh['light'=8,'view'=64] {'light'}, dimensions={0} | all-to-all | bytes 524288 | tf_op jit(solution)/shard_map/all_to_all | solution.py:270
  18.9 4.4 %propagate.1 = bf16[8,3,2,8,256]{4,3,2,1,0:T(8,128)(2,1)} custom-call(bf16[8,4,2,8,256]{4,3,2,1,0:T(8,128)(2,1)} %all_to_all.20.recv_ref, f32[3,2,8,256]{3,2,1,0:T(8,128)} %get-tuple-element.14.rows_ref, f32[4,4]{1,0:T(4,128)} %refs_5_.1, f32[3]{0:T(128)} %absorb_ref.3), custom_call_target="tpu_custom_call" | custom-call | tf_op jit(solution)/shard_map/propagate/pallas_call | solution.py:284
  23.3 6.6 %all-to-all-start.1 = ((bf16[8,3,2,8,256]{4,3,2,1,0:T(8,128)(2,1)}), bf16[8,3,2,8,256]{4,3,2,1,0:T(8,128)(2,1)S(1)}, u32[]{:S(2)}, u32[]{:S(2)}) async-start(bf16[8,3,2,8,256]{4,3,2,1,0:T(8,128)(2,1)} %propagate.1), calls=%async_computation.1 | async-start | bytes 393216 | tf_op jit(solution)/shard_map/all_to_all | solution.py:291
  29.9 4.6 %collective-permute-start = (bf16[16,8,256]{2,1,0:T(8,128)(2,1)}, bf16[16,8,256]{2,1,0:T(8,128)(2,1)S(1)}, u32[]{:S(2)}, u32[]{:S(2)}) collective-permute-start(bf16[16,8,256]{2,1,0:T(8,128)(2,1)} %get-tuple-element.16), channel_id=1, source_target_pairs={{0,64},{64,128},{128,192},{192,256},{256,320},{320,384},{384,448},... | collective-permute-start | bytes 196616 | tf_op jit(solution)/shard_map/ppermute | solution.py:268
  34.5 1.9 %collective-permute-start.1 = (bf16[16,8,256]{2,1,0:T(8,128)(2,1)}, bf16[16,8,256]{2,1,0:T(8,128)(2,1)S(1)}, u32[]{:S(2)}, u32[]{:S(2)}) collective-permute-start(bf16[16,8,256]{2,1,0:T(8,128)(2,1)} %get-tuple-element.17), channel_id=1, source_target_pairs={{64,0},{128,64},{192,128},{256,192},{320,256},{384,320},{448,384},... | collective-permute-start | bytes 196616 | tf_op jit(solution)/shard_map/ppermute | solution.py:269
  37.0 0.0 collective-permute-done.refs_1_
  37.0 0.0 copy-start.1
  37.1 5.0 %collective-permute-done.1.refs_2_ = bf16[16,8,256]{2,1,0:T(8,128)(2,1)S(1)} collective-permute-done((bf16[16,8,256]{2,1,0:T(8,128)(2,1)}, bf16[16,8,256]{2,1,0:T(8,128)(2,1)S(1)}, u32[]{:S(2)}, u32[]{:S(2)}) %collective-permute-start.1) | collective-permute-done | bytes 65568 | tf_op jit(solution)/shard_map/ppermute | solution.py:269
  42.0 0.0 copy-start.2
  42.0 0.0 copy-done.1
  42.0 0.6 copy-done.2
  42.7 4.5 %local.1 = (f32[4,16,8,256]{3,2,1,0:T(8,128)}, f32[4,16,3,8,256]{4,3,2,1,0:T(8,128)}, f32[4,4,8,256]{3,2,1,0:T(8,128)}) custom-call(bf16[4,16,8,256]{3,2,1,0:T(8,128)(2,1)} %get-tuple-element.15.refs_0_, bf16[16,8,256]{2,1,0:T(8,128)(2,1)} %copy-done.1, bf16[16,8,256]{2,1,0:T(8,128)(2,1)} %copy-done.2, s32[1,1,16]{2,1,0:T(1,128)} %refs_3_.1, ...), custom_call_target="tpu_custom_call" | custom-call | tf_op jit(solution)/shard_map/local/pallas_call | solution.py:272
  47.2 0.0 all-to-all-done.1.front_ref
  47.2 0.0 copy-start
  47.2 0.7 copy-done
  47.8 4.6 %shade.1 = f32[8,4,8,128]{3,2,1,0:T(8,128)} custom-call(bf16[8,3,2,8,256]{4,3,2,1,0:T(8,128)(2,1)} %copy-done, f32[4,16,8,256]{3,2,1,0:T(8,128)} %get-tuple-element.18.ext_ref, f32[4,16,3,8,256]{4,3,2,1,0:T(8,128)} %get-tuple-element.19.gain_ref, f32[4,4,8,256]{3,2,1,0:T(8,128)} %get-tuple-element.20.base_ref, f32[3]{0:T(128)} %absorb_ref.3), custom_call_target="tpu_custom_call" | custom-call | tf_op jit(solution)/shard_map/shade/pallas_call | solution.py:293
  52.5 10.1 %all_to_all.21.parts_ref = f32[8,4,8,128]{3,2,1,0:T(8,128)} all-to-all(f32[8,4,8,128]{3,2,1,0:T(8,128)} %shade.1), channel_id=1, replica_groups={{0,1,2,3,4,5,6,7},{8,9,10,11,12,13,14,15},{16,17,18,19,20,21,22,23},{24..., dimensions={0} | all-to-all | bytes 262144 | tf_op jit(solution)/shard_map/all_to_all | solution.py:304
  62.6 1.5 %merge.1 = f32[8,4,128]{2,1,0:T(4,128)} custom-call(f32[8,4,8,128]{3,2,1,0:T(8,128)} %all_to_all.21.parts_ref, f32[1]{0:T(128)S(6)} %copy.7.refs_4_.sign_ref), custom_call_target="tpu_custom_call" | custom-call | tf_op jit(solution)/shard_map/merge/pallas_call | solution.py:305
  64.1 17.8 %all_to_all.22.parts_ref = f32[8,4,128]{2,1,0:T(4,128)} all-to-all(f32[8,4,128]{2,1,0:T(4,128)} %merge.1), channel_id=1, replica_groups={{0,8,16,24,32,40,48,56},{1,9,17,25,33,41,49,57},{2,10,18,26,34,42,50,58..., dimensions={0} | all-to-all | bytes 32768 | tf_op jit(solution)/shard_map/all_to_all | solution.py:312
  81.9 1.3 %final.1 = f32[4,128]{1,0:T(4,128)} custom-call(f32[8,4,128]{2,1,0:T(4,128)} %all_to_all.22.parts_ref, f32[1]{0:T(128)S(6)} %copy.7.refs_4_.sign_ref), custom_call_target="tpu_custom_call" | custom-call | tf_op jit(solution)/shard_map/final/pallas_call | solution.py:313
Async XLA Ops:
  23.3 23.9 %all-to-all-start.1 = ((bf16[8,3,2,8,256]{4,3,2,1,0:T(8,128)(2,1)}), bf16[8,3,2,8,256]{4,3,2,1,0:T(8,128)(2,1)S(1)}, u32[]{:S(2)}, u32[]{:S(2)}) async-start(bf16[8,3,2,8,256]{4,3,2,1,0:T(8,128)(2,1)} %propagate.1), calls=%async_computation.1 | async-start | bytes 393216 | tf_op jit(solution)/shard_map/all_to_all | solution.py:291
  29.9 7.2 %collective-permute-start = (bf16[16,8,256]{2,1,0:T(8,128)(2,1)}, bf16[16,8,256]{2,1,0:T(8,128)(2,1)S(1)}, u32[]{:S(2)}, u32[]{:S(2)}) collective-permute-start(bf16[16,8,256]{2,1,0:T(8,128)(2,1)} %get-tuple-element.16), channel_id=1, source_target_pairs={{0,64},{64,128},{128,192},{192,256},{256,320},{320,384},{384,448},... | collective-permute-start | bytes 196616 | tf_op jit(solution)/shard_map/ppermute | solution.py:268
  34.5 7.6 %collective-permute-start.1 = (bf16[16,8,256]{2,1,0:T(8,128)(2,1)}, bf16[16,8,256]{2,1,0:T(8,128)(2,1)S(1)}, u32[]{:S(2)}, u32[]{:S(2)}) collective-permute-start(bf16[16,8,256]{2,1,0:T(8,128)(2,1)} %get-tuple-element.17), channel_id=1, source_target_pairs={{64,0},{128,64},{192,128},{256,192},{320,256},{384,320},{448,384},... | collective-permute-start | bytes 196616 | tf_op jit(solution)/shard_map/ppermute | solution.py:269
  37.0 5.0 %copy-start.1 = (bf16[16,8,256]{2,1,0:T(8,128)(2,1)}, bf16[16,8,256]{2,1,0:T(8,128)(2,1)S(1)}, u32[]{:S(2)}) copy-start(bf16[16,8,256]{2,1,0:T(8,128)(2,1)S(1)} %collective-permute-done.refs_1_) | copy-start | bytes 196612
  42.0 0.6 copy-start.2
  47.2 0.7 copy-start

commit v2 on v1

--- a/solution.py
+++ b/solution.py
@@ -5,12 +5,14 @@
 from jax.experimental.pallas import tpu as pltpu
 from jax.sharding import PartitionSpec as P
 
+
 S = 8
 T = 256
 H = 128
 F32 = jnp.float32
 BF16 = jnp.bfloat16
 VMEM = pl.BlockSpec(memory_space=pltpu.VMEM)
+LIMIT = pltpu.CompilerParams(vmem_limit_bytes=16 << 20)
 SMEM = pl.BlockSpec(memory_space=pltpu.SMEM)
 
 
@@ -67,7 +69,7 @@
     return out
 
 
-def prepare_kernel(dens_ref, occ_ref, light_ref, pos_ref, cells_ref, first_ref, last_ref, send_ref, rows_ref, tmp):
+def prepare_kernel(dens_ref, occ_ref, cells_ref, first_ref, last_ref, send_ref, tmp):
     layers, rows, _ = dens_ref.shape
     occ = brick_mask(occ_ref)
     mask = jnp.concatenate(occ, axis=1)[None] > 0.5
@@ -86,11 +88,6 @@
             last_ref[...] = raw
         masked = jnp.where(mask, y, -1.0).astype(BF16)
         send_ref[:, layer] = masked.reshape(rows // 2, 2, S, T)
-    start = 2 * pos_ref[0]
-    for c in range(3):
-        for r in range(2):
-            for s in range(S):
-                rows_ref[c, r, s : s + 1, :] = light_ref[c, pl.ds(start + r, 1), s * T : (s + 1) * T]
 
 
 def propagate_kernel(recv_ref, rows_ref, transfer_ref, absorb_ref, send_ref):
@@ -119,7 +116,15 @@
         send_ref[blocks - 1, c, :, :, H:] = final[c][1].astype(BF16)
 
 
-def local_kernel(cells_ref, low_ref, high_ref, occ_ref, sign_ref, transfer_ref, ext_ref, gain_ref, base_ref, *, total_y):
+def local_kernel(
+    cells_ref, low_ref, high_ref, light_ref, occ_ref, sign_ref, transfer_ref, pos_ref,
+    ext_ref, gain_ref, base_ref, rows_ref, *, total_y,
+):
+    start = 2 * pos_ref[0]
+    for c in range(3):
+        for r in range(2):
+            for s in range(S):
+                rows_ref[c, r, s : s + 1, :] = light_ref[c, pl.ds(start + r, 1), s * T : (s + 1) * T]
     layers, rows = cells_ref.shape[0], cells_ref.shape[1]
     occ = brick_mask(occ_ref)
     sign = sign_ref[0]
@@ -179,7 +184,7 @@
             base_ref[layer, 3, :, h * H : (h + 1) * H] = 1.0 - through[h]
 
 
-def shade_kernel(front_ref, ext_ref, gain_ref, base_ref, absorb_ref, send_ref, tmp):
+def shade_kernel(front_ref, ext_ref, gain_ref, base_ref, absorb_ref, send_ref):
     layers, rows = ext_ref.shape[0], ext_ref.shape[1]
     scale = [-absorb_ref[c] / 32.0 for c in range(3)]
 
@@ -206,117 +211,104 @@
     for layer in range(layers):
         for h in range(2):
             for c in range(4):
-                if c < 3:
-                    tmp[layer, c, h] = final[layer][2 * c + h]
-                else:
-                    tmp[layer, c, h] = base_ref[layer, 3, :, h * H : (h + 1) * H]
-                for j in range(4):
-                    send_ref[2 * j + h, c, 2 * layer : 2 * layer + 2, :] = tmp[layer, c, h, pl.ds(j, 2, stride=4), :]
-
-
-def merge_kernel(parts_ref, sign_ref, send_ref):
-    count = parts_ref.shape[0]
+                value = final[layer][2 * c + h] if c < 3 else base_ref[layer, 3, :, h * H : (h + 1) * H]
+                send_ref[pl.ds(layer * 64 + h * 4 + c, S, stride=8), :] = value
+
+
+def merge_kernel(parts_ref, sign_ref, out_ref):
     back = sign_ref[0] < 0.0
-    through, colour = None, None
-    for i in range(count):
-        k = jnp.where(back, count - 1 - i, i)
-        part = [parts_ref[k, c] for c in range(4)]
-        if colour is None:
-            colour, through = part[:3], 1.0 - part[3]
-        else:
-            colour = [colour[c] + through * part[c] for c in range(3)]
-            through = through * (1.0 - part[3])
-    for c in range(3):
-        send_ref[:, c, :] = colour[c]
-    send_ref[:, 3, :] = 1.0 - through
-
-
-def final_kernel(parts_ref, sign_ref, out_ref):
-    count = parts_ref.shape[0]
-    back = sign_ref[0] < 0.0
+
+    def over(near, far):
+        through = 1.0 - near[3]
+        return [near[c] + through * far[c] for c in range(4)]
+
     held = None
-    for i in range(count):
-        k = jnp.where(back, count - 1 - i, i)
-        part = parts_ref[k]
-        held = part if held is None else held + (1.0 - held[3:4]) * part
-    out_ref[...] = held
+    for i in range(8):
+        j = jnp.where(back, 7 - i, i)
+        part = [parts_ref[pl.ds(4 * j + c, 8, stride=32), :] for c in range(4)]
+        held = part if held is None else over(held, part)
+    for step in (1, 2, 4):
+        other = [pltpu.roll(x, 8 - step, 0) for x in held]
+        near = [jnp.where(back, o, h) for o, h in zip(other, held)]
+        far = [jnp.where(back, h, o) for o, h in zip(other, held)]
+        held = over(near, far)
+    for c in range(4):
+        out_ref[c : c + 1, :] = held[c][:1]
+
+
+def in_vmem(x):
+    return pltpu.with_memory_space_constraint(x, pltpu.VMEM)
 
 
 def body(density, occupied, view_sign, transfer, absorb, light_in):
-    layers, rows, columns = density.shape
+    layers, rows, _ = density.shape
     lights = lax.axis_size("light")
     views = lax.axis_size("view")
     pos = lax.axis_index("light").astype(jnp.int32)[None]
-    sds = jax.ShapeDtypeStruct
-
-    cells, first, last, send, light_rows = pl.pallas_call(
+    out = pltpu.VMEM
+
+    cells, first, last, send = pl.pallas_call(
         prepare_kernel,
         out_shape=(
-            sds((layers, rows, S, T), BF16),
-            sds((rows, S, T), BF16),
-            sds((rows, S, T), BF16),
-            sds((lights, layers, 2, S, T), BF16),
-            sds((3, 2, S, T), F32),
+            out((layers, rows, S, T), BF16),
+            out((rows, S, T), BF16),
+            out((rows, S, T), BF16),
+            out((lights, layers, 2, S, T), BF16),
         ),
-        in_specs=[VMEM, SMEM, VMEM, SMEM],
-        out_specs=(VMEM,) * 5,
+        in_specs=[VMEM, SMEM],
+        out_specs=(VMEM,) * 4,
         scratch_shapes=[pltpu.VMEM((2 * rows * S, H), F32)],
+        compiler_params=LIMIT,
         name="prepare",
-    )(density, occupied, light_in, pos)
+    )(density, occupied)
 
     ends = lights - 1
     low = lax.ppermute(last, "light", [(i, i + 1) for i in range(ends)])
     high = lax.ppermute(first, "light", [(i + 1, i) for i in range(ends)])
     recv = lax.all_to_all(send, "light", 0, 0)
 
-    ext, gain, base = pl.pallas_call(
+    ext, gain, base, light_rows = pl.pallas_call(
         lambda *refs: local_kernel(*refs, total_y=rows * views),
         out_shape=(
-            sds((layers, rows, S, T), F32),
-            sds((layers, rows, 3, S, T), F32),
-            sds((layers, 4, S, T), F32),
+            out((layers, rows, S, T), F32),
+            out((layers, rows, 3, S, T), F32),
+            out((layers, 4, S, T), F32),
+            out((3, 2, S, T), F32),
         ),
-        in_specs=[VMEM, VMEM, VMEM, SMEM, SMEM, SMEM],
-        out_specs=(VMEM,) * 3,
+        in_specs=[VMEM, VMEM, VMEM, VMEM, SMEM, SMEM, SMEM, SMEM],
+        out_specs=(VMEM,) * 4,
+        compiler_params=LIMIT,
         name="local",
-    )(cells, low, high, occupied, view_sign, transfer)
+    )(in_vmem(cells), in_vmem(low), in_vmem(high), light_in, occupied, view_sign, transfer, pos)
 
     fronts = pl.pallas_call(
         propagate_kernel,
-        out_shape=sds((lights, 3, 2, S, T), BF16),
+        out_shape=out((lights, 3, 2, S, T), BF16),
         in_specs=[VMEM, VMEM, SMEM, SMEM],
         out_specs=VMEM,
+        compiler_params=LIMIT,
         name="propagate",
-    )(recv, light_rows, transfer, absorb)
+    )(in_vmem(recv), in_vmem(light_rows), transfer, absorb)
     front = lax.all_to_all(fronts, "light", 0, 0)
 
     partial = pl.pallas_call(
         shade_kernel,
-        out_shape=sds((8, 4, 8, H), F32),
+        out_shape=out((views * 4, H), F32),
         in_specs=[VMEM, VMEM, VMEM, VMEM, SMEM],
         out_specs=VMEM,
-        scratch_shapes=[pltpu.VMEM((layers, 4, 2, S, H), F32)],
+        compiler_params=LIMIT,
         name="shade",
-    )(front, ext, gain, base, absorb)
-
-    near = [[z * 8 + k for k in range(8)] for z in range(views // 8)]
-    far = [[z * 8 + k for z in range(views // 8)] for k in range(8)]
-    parts = lax.all_to_all(partial, "view", 0, 0, axis_index_groups=near)
-    merged = pl.pallas_call(
+    )(in_vmem(front), in_vmem(ext), in_vmem(gain), in_vmem(base), absorb)
+
+    parts = lax.all_to_all(partial.reshape(views, 4, H), "view", 0, 0).reshape(views * 4, H)
+    return pl.pallas_call(
         merge_kernel,
-        out_shape=sds((8, 4, H), F32),
+        out_shape=jax.ShapeDtypeStruct((4, H), F32),
         in_specs=[VMEM, SMEM],
         out_specs=VMEM,
+        compiler_params=LIMIT,
         name="merge",
-    )(parts, view_sign)
-    parts = lax.all_to_all(merged, "view", 0, 0, axis_index_groups=far)
-    return pl.pallas_call(
-        final_kernel,
-        out_shape=sds((4, H), F32),
-        in_specs=[VMEM, SMEM],
-        out_specs=VMEM,
-        name="final",
-    )(parts, view_sign)
+    )(in_vmem(parts), view_sign)
 
 
 def solution(mesh):

time: 83.9 us -> 74.8 us (0.89)
  the two profiles are of different devices: /device:TPU:24 before, /device:TPU:1 now
where the time goes in v2:
time: 74.8 us; the launch traced here: 74.4 us
  blocking collectives  42.9 us (57%)
  starting transfers between devices  12.3 us (16%)
  Pallas kernels  11 us (15%)
  local copies, waits for them, and re-layouts  3.94 us (5%)
  waiting for transfers between devices  3.61 us (5%)
    all_to_all x1, blocking collectives, body(): lax.all_to_all(partial.reshape(views, 4, H), 'view', 0, 0)  28.3 us
    all_to_all x1, blocking collectives, body(): front = lax.all_to_all(fronts, 'light', 0, 0)  14.6 us
    all_to_all x1, starting transfers between devices, body(): recv = lax.all_to_all(send, 'light', 0, 0)  7.64 us
    unnamed x14, local copies, waits for them, and re-layouts  3.94 us
    ppermute x1, starting transfers between devices, body(): low = lax.ppermute(last, 'light', [(i, i + 1) for i in range(ends)])  3.36 us
    pallas_call x1, Pallas kernels, body(): pl.pallas_call(propagate_kernel, out_shape=out((lights, 3, 2, S, T), BF16...  3.34 us
    ppermute x1, waiting for transfers between devices, body(): high = lax.ppermute(first, 'light', [(i + 1, i) for i in range(ends)])  3.32 us
    pallas_call x1, Pallas kernels, body(): pl.pallas_call(shade_kernel, out_shape=out((views * 4, H), F32), in_specs...  2.84 us
  transfers between devices with their start and end apart: 3, of which 2 were waited for; matrix products, arithmetic and copies ran while one was open for 0% of the time, Pallas kernels for 4%

profile of v2, /device:TPU:1, one launch (start us, length us, event | category | flops | bytes accessed | tf_op | source)
XLA Modules:
  0.0 74.4 jit_solution(4255520868046131475)
XLA Ops:
  0.0 0.0 copy-start.1
  0.0 0.9 %copy-done.1 = bf16[4,16,2048]{2,1,0:T(8,128)(2,1)S(1)} copy-done((bf16[4,16,2048]{2,1,0:T(8,128)(2,1)S(1)}, bf16[4,16,2048]{2,1,0:T(8,128)(2,1)}, u32[]{:S(2)}) %copy-start.1) | copy-done | bytes 262168
  1.0 0.0 copy-start.4
  1.0 0.7 copy-done.4
  1.6 0.0 copy-start.3
  1.6 0.0 copy-start.6
  1.6 1.4 %prepare.1 = (bf16[4,16,8,256]{3,2,1,0:T(8,128)(2,1)S(1)}, bf16[16,8,256]{2,1,0:T(8,128)(2,1)S(1)}, bf16[16,8,256]{2,1,0:T(8,128)(2,1)S(1)}, bf16[8,4,2,8,256]{4,3,2,1,0:T(8,128)(2,1)}) custom-call(bf16[4,16,2048]{2,1,0:T(8,128)(2,1)S(1)} %copy-done.1, s32[1,1,16]{2,1,0:T(1,128)S(1)} %copy-done.4), custom_call_target="tpu_custom_call" | custom-call | tf_op jit(solution)/shard_map/prepare/pallas_call | solution.py:250
  3.0 7.6 %all-to-all-start = ((bf16[8,4,2,8,256]{4,3,2,1,0:T(8,128)(2,1)}), bf16[8,4,2,8,256]{4,3,2,1,0:T(8,128)(2,1)S(1)}, u32[]{:S(2)}, u32[]{:S(2)}) async-start(bf16[8,4,2,8,256]{4,3,2,1,0:T(8,128)(2,1)} %get-tuple-element.13), calls=%async_computation | async-start | bytes 524288 | tf_op jit(solution)/shard_map/all_to_all | solution.py:268
  10.6 3.4 %collective-permute-start = (bf16[16,8,256]{2,1,0:T(8,128)(2,1)S(1)}, bf16[16,8,256]{2,1,0:T(8,128)(2,1)S(1)}, u32[]{:S(2)}, u32[]{:S(2)}) collective-permute-start(bf16[16,8,256]{2,1,0:T(8,128)(2,1)S(1)} %get-tuple-element.15), channel_id=1, source_target_pairs={{0,64},{64,128},{128,192},{192,256},{256,320},{320,384},{384,448},... | collective-permute-start | bytes 196616 | tf_op jit(solution)/shard_map/ppermute | solution.py:266
  14.0 1.3 %collective-permute-start.1 = (bf16[16,8,256]{2,1,0:T(8,128)(2,1)S(1)}, bf16[16,8,256]{2,1,0:T(8,128)(2,1)S(1)}, u32[]{:S(2)}, u32[]{:S(2)}) collective-permute-start(bf16[16,8,256]{2,1,0:T(8,128)(2,1)S(1)} %get-tuple-element.16), channel_id=1, source_target_pairs={{64,0},{128,64},{192,128},{256,192},{320,256},{384,320},{448,384},... | collective-permute-start | bytes 196616 | tf_op jit(solution)/shard_map/ppermute | solution.py:267
  15.9 0.3 collective-permute-done.refs_1_
  16.2 3.3 %collective-permute-done.1.refs_2_ = bf16[16,8,256]{2,1,0:T(8,128)(2,1)S(1)} collective-permute-done((bf16[16,8,256]{2,1,0:T(8,128)(2,1)S(1)}, bf16[16,8,256]{2,1,0:T(8,128)(2,1)S(1)}, u32[]{:S(2)}, u32[]{:S(2)}) %collective-permute-start.1) | collective-permute-done | bytes 65568 | tf_op jit(solution)/shard_map/ppermute | solution.py:267
  19.5 0.0 copy-start
  19.6 1.0 %copy-done = f32[3,16,2048]{2,1,0:T(8,128)S(1)} copy-done((f32[3,16,2048]{2,1,0:T(8,128)S(1)}, f32[3,16,2048]{2,1,0:T(8,128)}, u32[]{:S(2)}) %copy-start) | copy-done | bytes 393240
  20.5 0.0 copy-start.2
  20.5 0.7 copy-done.2
  21.2 0.0 copy-start.5
  21.2 0.7 copy-done.5
  21.9 2.7 %local.1 = (f32[4,16,8,256]{3,2,1,0:T(8,128)S(1)}, f32[4,16,3,8,256]{4,3,2,1,0:T(8,128)S(1)}, f32[4,4,8,256]{3,2,1,0:T(8,128)S(1)}, f32[3,2,8,256]{3,2,1,0:T(8,128)S(1)}) custom-call(bf16[4,16,8,256]{3,2,1,0:T(8,128)(2,1)S(1)} %get-tuple-element.14.refs_0_, bf16[16,8,256]{2,1,0:T(8,128)(2,1)S(1)} %collective-permute-done.refs_1_, ...), custom_call_target="tpu_custom_call" | custom-call | tf_op jit(solution)/shard_map/local/pallas_call | solution.py:270
  24.6 0.0 all-to-all-done.recv_ref
  24.6 0.0 copy-done.3
  24.6 0.0 copy-done.6
  24.7 3.3 %propagate.1 = bf16[8,3,2,8,256]{4,3,2,1,0:T(8,128)(2,1)S(1)} custom-call(bf16[8,4,2,8,256]{4,3,2,1,0:T(8,128)(2,1)S(1)} %all-to-all-done.recv_ref, f32[3,2,8,256]{3,2,1,0:T(8,128)S(1)} %get-tuple-element.17.rows_ref, f32[4,4]{1,0:T(4,128)S(1)} %copy-done.3, f32[3]{0:T(128)S(1)} %copy-done.6), custom_call_target="tpu_custom_call" | custom-call | tf_op jit(solution)/shard_map/propagate/pallas_call | solution.py:284
  28.0 14.6 %all_to_all.15.front_ref = bf16[8,3,2,8,256]{4,3,2,1,0:T(8,128)(2,1)S(1)} all-to-all(bf16[8,3,2,8,256]{4,3,2,1,0:T(8,128)(2,1)S(1)} %propagate.1), channel_id=1, replica_groups=mesh['light'=8,'view'=64] {'light'}, dimensions={0} | all-to-all | bytes 393216 | tf_op jit(solution)/shard_map/all_to_all | solution.py:292
  42.6 2.8 %shade.1 = f32[256,128]{1,0:T(8,128)S(1)} custom-call(bf16[8,3,2,8,256]{4,3,2,1,0:T(8,128)(2,1)S(1)} %all_to_all.15.front_ref, f32[4,16,8,256]{3,2,1,0:T(8,128)S(1)} %get-tuple-element.18.ext_ref, f32[4,16,3,8,256]{4,3,2,1,0:T(8,128)S(1)} %get-tuple-element.19.gain_ref, f32[4,4,8,256]{3,2,1,0:T(8,128)S(1)} %get-tuple-element.20.base_ref, f32[3]{0:T(128)S(1)} %copy-done.6), custom_call_target="tpu_custom_call" | custom-call | tf_op jit(solution)/shard_map/shade/pallas_call | solution.py:294
  45.4 28.3 %all_to_all.16 = f32[64,4,128]{2,1,0:T(4,128)S(1)} all-to-all(f32[64,4,128]{2,1,0:T(4,128)S(1)} %bitcast.3), channel_id=1, replica_groups=mesh['light'=8,'view'=64] {'view'}, dimensions={0} | all-to-all | bytes 262144 | tf_op jit(solution)/shard_map/all_to_all | solution.py:303
  73.7 0.7 merge.1
Async XLA Ops:
  0.0 0.9 %copy-start.1 = (bf16[4,16,2048]{2,1,0:T(8,128)(2,1)S(1)}, bf16[4,16,2048]{2,1,0:T(8,128)(2,1)}, u32[]{:S(2)}) copy-start(bf16[4,16,2048]{2,1,0:T(8,128)(2,1)} %dens_ref.1) | copy-start | bytes 786436
  1.0 0.7 copy-start.4
  1.6 23.0 %copy-start.3 = (f32[4,4]{1,0:T(4,128)S(1)}, f32[4,4]{1,0:T(4,128)}, u32[]{:S(2)}) copy-start(f32[4,4]{1,0:T(4,128)} %transfer_ref.1) | copy-start | bytes 196
  1.6 23.0 %copy-start.6 = (f32[3]{0:T(128)S(1)}, f32[3]{0:T(128)}, u32[]{:S(2)}) copy-start(f32[3]{0:T(128)} %absorb_ref.3) | copy-start | bytes 40
  3.0 21.6 %all-to-all-start = ((bf16[8,4,2,8,256]{4,3,2,1,0:T(8,128)(2,1)}), bf16[8,4,2,8,256]{4,3,2,1,0:T(8,128)(2,1)S(1)}, u32[]{:S(2)}, u32[]{:S(2)}) async-start(bf16[8,4,2,8,256]{4,3,2,1,0:T(8,128)(2,1)} %get-tuple-element.13), calls=%async_computation | async-start | bytes 524288 | tf_op jit(solution)/shard_map/all_to_all | solution.py:268
  10.6 5.6 %collective-permute-start = (bf16[16,8,256]{2,1,0:T(8,128)(2,1)S(1)}, bf16[16,8,256]{2,1,0:T(8,128)(2,1)S(1)}, u32[]{:S(2)}, u32[]{:S(2)}) collective-permute-start(bf16[16,8,256]{2,1,0:T(8,128)(2,1)S(1)} %get-tuple-element.15), channel_id=1, source_target_pairs={{0,64},{64,128},{128,192},{192,256},{256,320},{320,384},{384,448},... | collective-permute-start | bytes 196616 | tf_op jit(solution)/shard_map/ppermute | solution.py:266
  14.0 5.6 %collective-permute-start.1 = (bf16[16,8,256]{2,1,0:T(8,128)(2,1)S(1)}, bf16[16,8,256]{2,1,0:T(8,128)(2,1)S(1)}, u32[]{:S(2)}, u32[]{:S(2)}) collective-permute-start(bf16[16,8,256]{2,1,0:T(8,128)(2,1)S(1)} %get-tuple-element.16), channel_id=1, source_target_pairs={{64,0},{128,64},{192,128},{256,192},{320,256},{384,320},{448,384},... | collective-permute-start | bytes 196616 | tf_op jit(solution)/shard_map/ppermute | solution.py:267
  19.5 1.0 %copy-start = (f32[3,16,2048]{2,1,0:T(8,128)S(1)}, f32[3,16,2048]{2,1,0:T(8,128)}, u32[]{:S(2)}) copy-start(f32[3,16,2048]{2,1,0:T(8,128)} %refs_3_.1) | copy-start | bytes 1179652
  20.5 0.7 copy-start.2
  21.2 0.7 copy-start.5

commit v3 on v2

v3 whole, which is shorter than its diff:
```python
import jax
import jax.numpy as jnp
from jax import lax
from jax.experimental import pallas as pl
from jax.experimental.pallas import tpu as pltpu
from jax.sharding import PartitionSpec as P

S = 8
T = 256
H = 128
F32 = jnp.float32
BF16 = jnp.bfloat16
VMEM = pl.BlockSpec(memory_space=pltpu.VMEM)
ANY = pl.BlockSpec(memory_space=pl.ANY)
LIMIT = pltpu.CompilerParams(vmem_limit_bytes=16 << 20)
SMEM = pl.BlockSpec(memory_space=pltpu.SMEM)


def halves(x):
    return x[..., :H], x[..., H:]


def shifted(a, b, by, fill=0.0):
    ra, rb = pltpu.roll(a, by % H, a.ndim - 1), pltpu.roll(b, by % H, a.ndim - 1)
    lane = lax.broadcasted_iota(jnp.int32, (S, H), 1)
    sub = lax.broadcasted_iota(jnp.int32, (S, H), 0)
    if by > 0:
        wrap = jnp.where(sub == 0, fill, pltpu.roll(rb, 1, a.ndim - 2))
        return jnp.where(lane < by, wrap, ra), jnp.where(lane < by, ra, rb)
    wrap = jnp.where(sub == S - 1, fill, pltpu.roll(ra, S - 1, a.ndim - 2))
    return jnp.where(lane >= H + by, rb, ra), jnp.where(lane >= H + by, wrap, rb)


def tap(before, cell, after):
    return [0.25 * (p + n) + 0.5 * c for p, c, n in zip(before, cell, after)]


def blur(a, b):
    return tap(shifted(a, b, 1), (a, b), shifted(a, b, -1))


ABSORB, PATH, OCCUPANCY, PLANES = 16, 19, 20, 22


def polynomial(const_ref, row, s):
    c = [const_ref[4 * row + n] for n in range(4)]
    return c[0] + s * (c[1] + s * (c[2] + s * c[3]))


def softplus(x):
    u = jnp.exp(-jnp.abs(x))
    tail = jnp.where(u < 2.0**-8, u * (1.0 - u * (0.5 - u * (1.0 / 3.0))), jnp.log(1.0 + u))
    return jnp.maximum(x, 0.0) + tail


def brick_mask(occ_ref):
    sub = lax.broadcasted_iota(jnp.int32, (S, H), 0)
    out = []
    for h in range(2):
        occ = jnp.zeros((S, H), F32)
        for s in range(S):
            occ = jnp.where(sub == s, occ_ref[0, 0, 2 * s + h].astype(F32), occ)
        out.append(occ)
    return out


TINY = 2.0**-100


def prepare_kernel(
    dens_ref, occ_hbm, transfer_hbm, absorb_hbm, sign_ref, cells_ref, const_ref, send_ref,
    raw, packed, tmp, occ_ref, transfer_ref, absorb_ref, in_sem, out_sem, small_sem, *, total_y,
):
    layers, rows, _ = dens_ref.shape
    small = [
        pltpu.make_async_copy(src, dst, small_sem.at[n])
        for n, (src, dst) in enumerate(
            ((occ_hbm, occ_ref), (transfer_hbm, transfer_ref), (absorb_hbm, absorb_ref))
        )
    ]
    loads = [pltpu.make_async_copy(dens_ref.at[n], raw.at[n], in_sem.at[n]) for n in range(layers)]
    stores = [pltpu.make_async_copy(packed.at[:, n], send_ref.at[:, n], out_sem.at[n]) for n in range(layers)]
    for copy in small[:1] + loads + small[1:]:
        copy.start()
    small[0].wait()
    occ = brick_mask(occ_ref)
    mask = jnp.concatenate(occ, axis=1)[None] > 0.5
    for layer in range(layers):
        loads[layer].wait()
        x = raw[layer].astype(F32)
        for s in range(S):
            for h in range(2):
                column = (2 * s + h) * H
                tmp[layer, h, pl.ds(s, rows, stride=S), :] = x[:, column : column + H]
        y = jnp.concatenate([tmp[layer, h].reshape(rows, S, H) for h in range(2)], axis=2)
        cells_ref[layer] = y.astype(BF16)
        sent = jnp.where(mask, y, -jnp.maximum(y, TINY)).astype(BF16)
        packed[:, layer] = sent.reshape(rows // 2, 2, S, T)
        stores[layer].start()
    for copy in small[1:]:
        copy.wait()
    for row in range(4):
        for n in range(4):
            const_ref[4 * row + n] = jnp.full((S, H), transfer_ref[row, n], F32)
    for c in range(3):
        const_ref[ABSORB + c] = jnp.full((S, H), absorb_ref[c] * (-1.0 / 32.0), F32)
    const_ref[PATH] = (2.0 / total_y) / jnp.abs(jnp.full((S, H), sign_ref[0], F32))
    for h in range(2):
        const_ref[OCCUPANCY + h] = occ[h]
    for store in stores:
        store.wait()


def propagate_kernel(recv_ref, rows_ref, const_ref, send_ref):
    blocks, layers = recv_ref.shape[0], recv_ref.shape[1]
    scale = [const_ref[ABSORB + c] for c in range(3)]

    def density(k, layer):
        d = recv_ref[k, layer].astype(F32)
        return jnp.where(d >= 0.0, d, jnp.where(d > -2.0 * TINY, 0.0, -d)).astype(BF16)

    for k in range(blocks):
        send_ref[k, 3] = density(k - 1, layers - 1) if k > 0 else jnp.zeros((2, S, T), BF16)
        send_ref[k, 4] = density(k + 1, 0) if k < blocks - 1 else jnp.zeros((2, S, T), BF16)

    def extinction(k):
        out = []
        for layer in range(layers):
            for d in halves(recv_ref[k, layer].astype(F32)):
                out.append(jnp.where(d < 0.0, 0.0, softplus(polynomial(const_ref, 0, d))))
        return tuple(out)

    def emit(k, front):
        for c in range(3):
            send_ref[k, c, :, :, :H] = front[2 * c].astype(BF16)
            send_ref[k, c, :, :, H:] = front[2 * c + 1].astype(BF16)

    def block(k, carry):
        front, ext = list(carry[0]), carry[1]
        emit(k, front)
        for first in range(0, layers, 2):
            here, then = ext[2 * first : 2 * first + 2], ext[2 * first + 2 : 2 * first + 4]
            sides = [shifted(*then, 1, fill=1e30), then, shifted(*then, -1, fill=1e30)]
            for c in range(3):
                g = [f * jnp.exp(scale[c] * e) for f, e in zip(front[2 * c : 2 * c + 2], here)]
                g = [shifted(*g, 2), shifted(*g, 1), g, shifted(*g, -1), shifted(*g, -2)]
                lit = []
                for n in range(3):
                    arrived = tap(g[n], g[n + 1], g[n + 2])
                    lit.append([f * jnp.exp(scale[c] * e) for f, e in zip(arrived, sides[n])])
                front[2 * c : 2 * c + 2] = tap(*lit)
        return tuple(front), extinction(k + 1)

    init = tuple(x for c in range(3) for x in halves(rows_ref[c]))
    front, _ = lax.fori_loop(0, blocks - 1, block, (init, extinction(0)))
    emit(blocks - 1, front)


def local_kernel(
    cells_ref, light_ref, const_ref, sign_ref,
    ext_ref, gain_ref, slope_ref, base_ref, rows_ref, light, sem,
):
    layers, rows = cells_ref.shape[0], cells_ref.shape[1]
    load = pltpu.make_async_copy(light_ref, light, sem)
    load.start()
    occ = [const_ref[OCCUPANCY + h] for h in range(2)]
    back = sign_ref[0] < 0.0
    path = const_ref[PATH]

    def row(i, carry):
        r = jnp.where(back, rows - 1 - i, i)
        up = jnp.minimum(r + 1, rows - 1)
        down = jnp.maximum(r - 1, 0)
        column = [halves(cells_ref[layer, r].astype(F32)) for layer in range(layers)]
        new = []
        for layer in range(layers):
            through, base = carry[layer]
            d = column[layer]
            dn = halves(cells_ref[layer, up].astype(F32))
            dp = halves(cells_ref[layer, down].astype(F32))
            zp, zn = shifted(*d, 1), shifted(*d, -1)
            t_out, b_out = [], []
            for h in range(2):
                at = slice(h * H, (h + 1) * H)
                s = d[h]
                gy = 0.5 * (dn[h] - dp[h])
                gz = 0.5 * (zn[h] - zp[h])
                side, length = 0.36 * gy + 0.48 * gz, 1.0 + gy * gy + gz * gz
                if 0 < layer < layers - 1:
                    gx = 0.5 * (column[layer + 1][h] - column[layer - 1][h])
                    shading = 0.65 + 0.35 * ((0.8 * gx + side) * lax.rsqrt(length + gx * gx))
                else:
                    edge = 0 if layer == 0 else 1
                    slope_ref[edge, 0, r, :, at] = side
                    slope_ref[edge, 1, r, :, at] = length
                    shading = None
                ext = softplus(polynomial(const_ref, 0, s)) * occ[h]
                ext_ref[layer, r, :, at] = ext
                passing = jnp.exp(-ext * path)
                weight = through[h] * (1.0 - passing)
                colours = []
                for c in range(3):
                    lit = weight * jax.nn.sigmoid(polynomial(const_ref, c + 1, s))
                    colours.append(base[h][c] + lit)
                    gain_ref[layer, r, c, :, at] = lit if shading is None else lit * shading
                b_out.append(tuple(colours))
                t_out.append(through[h] * passing)
            new.append((tuple(t_out), tuple(b_out)))
        return tuple(new)

    one, zero = jnp.ones((S, H), F32), jnp.zeros((S, H), F32)
    init = tuple(((one, one), ((zero,) * 3, (zero,) * 3)) for _ in range(layers))
    final = lax.fori_loop(0, rows, row, init)
    for layer in range(layers):
        through, base = final[layer]
        for h in range(2):
            for c in range(3):
                base_ref[layer, c, :, h * H : (h + 1) * H] = 0.2 * base[h][c]
            base_ref[layer, 3, :, h * H : (h + 1) * H] = 1.0 - through[h]
    load.wait()
    start = 2 * lax.axis_index("light")
    for c in range(3):
        for r in range(2):
            for s in range(S):
                rows_ref[c, r, s : s + 1, :] = light[c, pl.ds(start + r, 1), s * T : (s + 1) * T]


def shade_kernel(front_ref, cells_ref, ext_ref, gain_ref, slope_ref, base_ref, const_ref, send_ref, shade):
    layers, rows = ext_ref.shape[0], ext_ref.shape[1]

    def finish(i, carry):
        for q in range(2):
            r = 2 * i + q
            for edge in range(2):
                low = front_ref[i, 3, q] if edge == 0 else cells_ref[layers - 2, r]
                high = cells_ref[1, r] if edge == 0 else front_ref[i, 4, q]
                gx = 0.5 * (high.astype(F32) - low.astype(F32))
                facing = (0.8 * gx + slope_ref[edge, 0, r]) * lax.rsqrt(slope_ref[edge, 1, r] + gx * gx)
                shade[edge, r] = 0.65 + 0.35 * facing
        return carry

    lax.fori_loop(0, rows // 2, finish, 0)

    def channel(c, carry):
        scale = const_ref[ABSORB + c]
        front = [halves(front_ref[r // 2, c, r % 2].astype(F32)) for r in range(rows)]
        for layer in range(layers):
            total = list(halves(base_ref[layer, c]))
            for r in range(rows):
                gain = halves(gain_ref[layer, r, c])
                if layer in (0, layers - 1):
                    gain = [g * s for g, s in zip(gain, halves(shade[min(layer, 1), r]))]
                total = [x + f * g for x, f, g in zip(total, front[r], gain)]
                if layer < layers - 1:
                    ext = halves(ext_ref[layer, r])
                    front[r] = blur(*[f * jnp.exp(scale * e) for f, e in zip(front[r], ext)])
            for h in range(2):
                send_ref[pl.ds(layer * 64 + h * 4 + c, S, stride=8), :] = total[h]
        return carry

    lax.fori_loop(0, 3, channel, 0)
    for layer in range(layers):
        for h in range(2):
            send_ref[pl.ds(layer * 64 + h * 4 + 3, S, stride=8), :] = base_ref[layer, 3, :, h * H : (h + 1) * H]


def merge_kernel(parts_ref, sign_ref, out_ref):
    back = sign_ref[0] < 0.0

    def over(near, far):
        through = 1.0 - near[3]
        return [near[c] + through * far[c] for c in range(4)]

    held = None
    for i in range(8):
        j = jnp.where(back, 7 - i, i)
        part = [parts_ref[pl.ds(4 * j + c, 8, stride=32), :] for c in range(4)]
        held = part if held is None else over(held, part)
    for step in (1, 2, 4):
        other = [pltpu.roll(x, 8 - step, 0) for x in held]
        near = [jnp.where(back, o, h) for o, h in zip(other, held)]
        far = [jnp.where(back, h, o) for o, h in zip(other, held)]
        held = over(near, far)
    for c in range(4):
        out_ref[c : c + 1, :] = held[c][:1]


def in_vmem(x):
    return pltpu.with_memory_space_constraint(x, pltpu.VMEM)


def in_hbm(x):
    return pltpu.with_memory_space_constraint(x, pltpu.HBM)


def body(density, occupied, view_sign, transfer, absorb, light_in):
    layers, rows, columns = density.shape
    lights = lax.axis_size("light")
    views = lax.axis_size("view")
    out = pltpu.VMEM
    small = (occupied, transfer, absorb)

    cells, const, send = pl.pallas_call(
        lambda *refs: prepare_kernel(*refs, total_y=rows * views),
        out_shape=(
            out((layers, rows, S, T), BF16),
            out((PLANES, S, H), F32),
            pltpu.HBM((lights, layers, 2, S, T), BF16),
        ),
        in_specs=[ANY] * 4 + [SMEM],
        out_specs=(VMEM, VMEM, ANY),
        scratch_shapes=[
            pltpu.VMEM((layers, rows, columns), BF16),
            pltpu.VMEM((lights, layers, 2, S, T), BF16),
            pltpu.VMEM((layers, 2, rows * S, H), F32),
            *[pltpu.SMEM(x.shape, x.dtype) for x in small],
            pltpu.SemaphoreType.DMA((layers,)),
            pltpu.SemaphoreType.DMA((layers,)),
            pltpu.SemaphoreType.DMA((len(small),)),
        ],
        compiler_params=LIMIT,
        name="prepare",
    )(*[in_hbm(x) for x in (density, *small)], view_sign)
    const = in_vmem(const)

    recv = lax.all_to_all(send, "light", 0, 0)

    ext, gain, slope, base, light_rows = pl.pallas_call(
        local_kernel,
        out_shape=(
            out((layers, rows, S, T), F32),
            out((layers, rows, 3, S, T), F32),
            out((2, 2, rows, S, T), F32),
            out((layers, 4, S, T), F32),
            out((3, 2, S, T), F32),
        ),
        in_specs=[VMEM, ANY, VMEM, SMEM],
        out_specs=(VMEM,) * 5,
        scratch_shapes=[pltpu.VMEM(light_in.shape, F32), pltpu.SemaphoreType.DMA(())],
        compiler_params=LIMIT,
        name="local",
    )(in_vmem(cells), in_hbm(light_in), const, view_sign)

    fronts = pl.pallas_call(
        propagate_kernel,
        out_shape=out((lights, 5, 2, S, T), BF16),
        in_specs=[VMEM, VMEM, VMEM],
        out_specs=VMEM,
        compiler_params=LIMIT,
        name="propagate",
    )(in_vmem(recv), in_vmem(light_rows), const)
    front = lax.all_to_all(fronts, "light", 0, 0)

    partial = pl.pallas_call(
        shade_kernel,
        out_shape=out((views * 4, H), F32),
        in_specs=[VMEM] * 7,
        out_specs=VMEM,
        scratch_shapes=[pltpu.VMEM((2, rows, S, T), F32)],
        compiler_params=LIMIT,
        name="shade",
    )(*[in_vmem(x) for x in (front, cells, ext, gain, slope, base)], const)

    parts = lax.all_to_all(partial.reshape(views, 4, H), "view", 0, 0).reshape(views * 4, H)
    return pl.pallas_call(
        merge_kernel,
        out_shape=jax.ShapeDtypeStruct((4, H), F32),
        in_specs=[VMEM, SMEM],
        out_specs=VMEM,
        compiler_params=LIMIT,
        name="merge",
    )(in_vmem(parts), view_sign)


def solution(mesh):
    in_specs = (
        P("light", "view", None),
        P("light", "view", None),
        P(),
        P(),
        P(),
        P(None, "view", None),
    )
    out_specs = P(None, ("light", "view"))
    return jax.shard_map(body, mesh=mesh, in_specs=in_specs, out_specs=out_specs, check_vma=False)
```

time: 74.8 us -> 65.9 us (0.88)
  starting transfers between devices: 12.3 us -> 7.65 us
  local copies, waits for them, and re-layouts: 3.94 us -> 0 us
  waiting for transfers between devices: 3.61 us -> 7.42 us
  Pallas kernels: 11 us -> 7.77 us
  blocking collectives: 42.9 us -> 42 us
    all_to_all x1, waiting for transfers between devices: 0.01 us -> 7.42 us  [body(): recv = lax.all_to_all(send, 'light', 0, 0)]
    ppermute x2 -> x0, starting transfers between devices: 4.65 us -> none  [the longest x1 3.36 us: body(): low = lax.ppermute(last, 'light', [(i, i + 1) for i in range(ends)])]
    unnamed x14 -> x0, local copies, waits for them, and re-layouts: 3.94 us -> none
    ppermute x2 -> x0, waiting for transfers between devices: 3.61 us -> none  [the longest x1 3.32 us: body(): high = lax.ppermute(first, 'light', [(i + 1, i) for i in range(ends)])]
    all_to_all x1, blocking collectives: 14.6 us -> 12.4 us  [body(): front = lax.all_to_all(fronts, 'light', 0, 0)]
    pallas_call x1, Pallas kernels: 2.84 us -> 1.11 us  [body(): pl.pallas_call(shade_kernel, out_shape=out((views * 4, H), F32), in_specs...]
    pallas_call x3, Pallas kernels: 7.45 us -> 5.97 us  [the longest x1 2.21 us: body(): pl.pallas_call(propagate_kernel, out_shape=out((lights, 5, 2, S, T), BF16...]
    all_to_all x1, blocking collectives: 28.3 us -> 29.6 us  [body(): lax.all_to_all(partial.reshape(views, 4, H), 'view', 0, 0)]
  transfers between devices with their start and end apart: 3 -> 1, of which waited for: 2 -> 1; matrix products, arithmetic and copies ran while one was open for 0% -> 0% of each run, Pallas kernels for 4% -> 3%
where the time goes in v3:
time: 65.9 us; the launch traced here: 65.5 us
  blocking collectives  42 us (64%)
  Pallas kernels  7.77 us (12%)
  starting transfers between devices  7.65 us (12%)
  waiting for transfers between devices  7.42 us (11%)
  between operations  0.69 us (1%)
    all_to_all x1, blocking collectives, body(): lax.all_to_all(partial.reshape(views, 4, H), 'view', 0, 0)  29.6 us
    all_to_all x1, blocking collectives, body(): front = lax.all_to_all(fronts, 'light', 0, 0)  12.4 us
    all_to_all x1, starting transfers between devices, body(): recv = lax.all_to_all(send, 'light', 0, 0)  7.65 us
    all_to_all x1, waiting for transfers between devices, body(): recv = lax.all_to_all(send, 'light', 0, 0)  7.42 us
    pallas_call x1, Pallas kernels, body(): pl.pallas_call(propagate_kernel, out_shape=out((lights, 5, 2, S, T), BF16...  2.21 us
    pallas_call x1, Pallas kernels, body(): pl.pallas_call(local_kernel, out_shape=(out((layers, rows, S, T), F32), o...  2.01 us
    pallas_call x1, Pallas kernels, body(): pl.pallas_call(lambda *refs: prepare_kernel(*refs, total_y=rows * views),...  1.75 us
  transfers between devices with their start and end apart: 1, of which 1 were waited for; matrix products, arithmetic and copies ran while one was open for 0% of the time, Pallas kernels for 3%

profile of v3, /device:TPU:1, one launch (start us, length us, event | category | flops | bytes accessed | tf_op | source)
XLA Modules:
  0.0 65.5 jit_solution(1592926167280176950)
XLA Ops:
  0.7 1.8 %prepare.1 = (bf16[4,16,8,256]{3,2,1,0:T(8,128)(2,1)S(1)}, f32[22,8,128]{2,1,0:T(8,128)S(1)}, bf16[8,4,2,8,256]{4,3,2,1,0:T(8,128)(2,1)}) custom-call(bf16[4,16,2048]{2,1,0:T(8,128)(2,1)} %refs_0_.1, s32[1,1,16]{2,1,0:T(1,128)} %refs_1_.1, f32[4,4]{1,0:T(4,128)} %refs_2_.1, f32[3]{0:T(128)} %refs_3_.1, f32[1]{0:T(128)S(6)} %copy.7.refs_4_.sign_ref), custom_call_target="tpu_custom_call" | custom-call | tf_op jit(solution)/shard_map/prepare/pallas_call | solution.py:303
  2.4 7.7 %all-to-all-start = ((bf16[8,4,2,8,256]{4,3,2,1,0:T(8,128)(2,1)}), bf16[8,4,2,8,256]{4,3,2,1,0:T(8,128)(2,1)S(1)}, u32[]{:S(2)}, u32[]{:S(2)}) async-start(bf16[8,4,2,8,256]{4,3,2,1,0:T(8,128)(2,1)} %get-tuple-element.13), calls=%async_computation | async-start | bytes 524288 | tf_op jit(solution)/shard_map/all_to_all | solution.py:326
  10.1 2.0 %local.1 = (f32[4,16,8,256]{3,2,1,0:T(8,128)S(1)}, f32[4,16,3,8,256]{4,3,2,1,0:T(8,128)S(1)}, f32[2,2,16,8,256]{4,3,2,1,0:T(8,128)S(1)}, f32[4,4,8,256]{3,2,1,0:T(8,128)S(1)}, f32[3,2,8,256]{3,2,1,0:T(8,128)S(1)}) custom-call(bf16[4,16,8,256]{3,2,1,0:T(8,128)(2,1)S(1)} %get-tuple-element.14.cells_ref, f32[3,16,2048]{2,1,0:T(8,128)} %light_ref.1, ...), custom_call_target="tpu_custom_call" | custom-call | tf_op jit(solution)/shard_map/local/pallas_call | solution.py:328
  12.1 7.4 %all-to-all-done.recv_ref = bf16[8,4,2,8,256]{4,3,2,1,0:T(8,128)(2,1)S(1)} async-done(((bf16[8,4,2,8,256]{4,3,2,1,0:T(8,128)(2,1)}), bf16[8,4,2,8,256]{4,3,2,1,0:T(8,128)(2,1)S(1)}, u32[]{:S(2)}, u32[]{:S(2)}) %all-to-all-start) | async-done | bytes 262176 | tf_op jit(solution)/shard_map/all_to_all | solution.py:326
  19.5 2.2 %propagate.1 = bf16[8,5,2,8,256]{4,3,2,1,0:T(8,128)(2,1)S(1)} custom-call(bf16[8,4,2,8,256]{4,3,2,1,0:T(8,128)(2,1)S(1)} %all-to-all-done.recv_ref, f32[3,2,8,256]{3,2,1,0:T(8,128)S(1)} %get-tuple-element.16.rows_ref, f32[22,8,128]{2,1,0:T(8,128)S(1)} %get-tuple-element.15.const_ref), custom_call_target="tpu_custom_call" | custom-call | tf_op jit(solution)/shard_map/propagate/pallas_call | solution.py:344
  21.7 12.4 %all_to_all.15.front_ref = bf16[8,5,2,8,256]{4,3,2,1,0:T(8,128)(2,1)S(1)} all-to-all(bf16[8,5,2,8,256]{4,3,2,1,0:T(8,128)(2,1)S(1)} %propagate.1), channel_id=1, replica_groups=mesh['light'=8,'view'=64] {'light'}, dimensions={0} | all-to-all | bytes 655360 | tf_op jit(solution)/shard_map/all_to_all | solution.py:352
  34.1 1.1 %shade.1 = f32[256,128]{1,0:T(8,128)S(1)} custom-call(bf16[8,5,2,8,256]{4,3,2,1,0:T(8,128)(2,1)S(1)} %all_to_all.15.front_ref, bf16[4,16,8,256]{3,2,1,0:T(8,128)(2,1)S(1)} %get-tuple-element.14.cells_ref, f32[4,16,8,256]{3,2,1,0:T(8,128)S(1)} %get-tuple-element.17.ext_ref, f32[4,16,3,8,256]{4,3,2,1,0:T(8,128)S(1)} %get-tuple-element.18.gain_ref, ...), custom_call_target="tpu_custom_call" | custom-call | tf_op jit(solution)/shard_map/shade/pallas_call | solution.py:354
  35.3 29.6 %all_to_all.16 = f32[64,4,128]{2,1,0:T(4,128)S(1)} all-to-all(f32[64,4,128]{2,1,0:T(4,128)S(1)} %bitcast.2), channel_id=1, replica_groups=mesh['light'=8,'view'=64] {'view'}, dimensions={0} | all-to-all | bytes 262144 | tf_op jit(solution)/shard_map/all_to_all | solution.py:364
  64.8 0.7 %merge.1 = f32[4,128]{1,0:T(4,128)} custom-call(f32[256,128]{1,0:T(8,128)S(1)} %bitcast.3, f32[1]{0:T(128)S(6)} %copy.7.refs_4_.sign_ref), custom_call_target="tpu_custom_call" | custom-call | tf_op jit(solution)/shard_map/merge/pallas_call | solution.py:365
Async XLA Ops:
  2.4 17.1 %all-to-all-start = ((bf16[8,4,2,8,256]{4,3,2,1,0:T(8,128)(2,1)}), bf16[8,4,2,8,256]{4,3,2,1,0:T(8,128)(2,1)S(1)}, u32[]{:S(2)}, u32[]{:S(2)}) async-start(bf16[8,4,2,8,256]{4,3,2,1,0:T(8,128)(2,1)} %get-tuple-element.13), calls=%async_computation | async-start | bytes 524288 | tf_op jit(solution)/shard_map/all_to_all | solution.py:326

commit v4 on v3

--- a/solution.py
+++ b/solution.py
@@ -16,6 +16,14 @@
 SMEM = pl.BlockSpec(memory_space=pltpu.SMEM)
 
 
+LIGHT_FIRST, LIGHT_STEP = 5, 1
+VIEW_TURN = 3
+
+
+def light_slot(k):
+    return (LIGHT_STEP * (k - LIGHT_FIRST)) & 7
+
+
 def halves(x):
     return x[..., :H], x[..., H:]
 
@@ -25,9 +33,9 @@
     lane = lax.broadcasted_iota(jnp.int32, (S, H), 1)
     sub = lax.broadcasted_iota(jnp.int32, (S, H), 0)
     if by > 0:
-        wrap = jnp.where(sub == 0, fill, pltpu.roll(rb, 1, a.ndim - 2))
+        wrap = jnp.where(sub == S - 1, fill, pltpu.roll(rb, S - 1, a.ndim - 2))
         return jnp.where(lane < by, wrap, ra), jnp.where(lane < by, ra, rb)
-    wrap = jnp.where(sub == S - 1, fill, pltpu.roll(ra, S - 1, a.ndim - 2))
+    wrap = jnp.where(sub == 0, fill, pltpu.roll(ra, 1, a.ndim - 2))
     return jnp.where(lane >= H + by, rb, ra), jnp.where(lane >= H + by, wrap, rb)
 
 
@@ -59,7 +67,7 @@
     for h in range(2):
         occ = jnp.zeros((S, H), F32)
         for s in range(S):
-            occ = jnp.where(sub == s, occ_ref[0, 0, 2 * s + h].astype(F32), occ)
+            occ = jnp.where(sub == s, occ_ref[0, 0, 2 * (S - 1 - s) + h].astype(F32), occ)
         out.append(occ)
     return out
 
@@ -90,12 +98,13 @@
         x = raw[layer].astype(F32)
         for s in range(S):
             for h in range(2):
-                column = (2 * s + h) * H
+                column = (2 * (S - 1 - s) + h) * H
                 tmp[layer, h, pl.ds(s, rows, stride=S), :] = x[:, column : column + H]
         y = jnp.concatenate([tmp[layer, h].reshape(rows, S, H) for h in range(2)], axis=2)
         cells_ref[layer] = y.astype(BF16)
         sent = jnp.where(mask, y, -jnp.maximum(y, TINY)).astype(BF16)
-        packed[:, layer] = sent.reshape(rows // 2, 2, S, T)
+        for k in range(rows // 2):
+            packed[light_slot(k), layer] = sent[2 * k : 2 * k + 2]
         stores[layer].start()
     for copy in small[1:]:
         copy.wait()
@@ -115,25 +124,26 @@
     blocks, layers = recv_ref.shape[0], recv_ref.shape[1]
     scale = [const_ref[ABSORB + c] for c in range(3)]
 
-    def density(k, layer):
-        d = recv_ref[k, layer].astype(F32)
+    def density(slot, layer):
+        d = recv_ref[slot, layer].astype(F32)
         return jnp.where(d >= 0.0, d, jnp.where(d > -2.0 * TINY, 0.0, -d)).astype(BF16)
 
     for k in range(blocks):
-        send_ref[k, 3] = density(k - 1, layers - 1) if k > 0 else jnp.zeros((2, S, T), BF16)
-        send_ref[k, 4] = density(k + 1, 0) if k < blocks - 1 else jnp.zeros((2, S, T), BF16)
+        slot, none = light_slot(k), jnp.zeros((2, S, T), BF16)
+        send_ref[slot, 3] = density(light_slot(k - 1), layers - 1) if k > 0 else none
+        send_ref[slot, 4] = density(light_slot(k + 1), 0) if k < blocks - 1 else none
 
     def extinction(k):
         out = []
         for layer in range(layers):
-            for d in halves(recv_ref[k, layer].astype(F32)):
+            for d in halves(recv_ref[light_slot(k), layer].astype(F32)):
                 out.append(jnp.where(d < 0.0, 0.0, softplus(polynomial(const_ref, 0, d))))
         return tuple(out)
 
     def emit(k, front):
         for c in range(3):
-            send_ref[k, c, :, :, :H] = front[2 * c].astype(BF16)
-            send_ref[k, c, :, :, H:] = front[2 * c + 1].astype(BF16)
+            send_ref[light_slot(k), c, :, :, :H] = front[2 * c].astype(BF16)
+            send_ref[light_slot(k), c, :, :, H:] = front[2 * c + 1].astype(BF16)
 
     def block(k, carry):
         front, ext = list(carry[0]), carry[1]
@@ -222,7 +232,11 @@
     for c in range(3):
         for r in range(2):
             for s in range(S):
-                rows_ref[c, r, s : s + 1, :] = light[c, pl.ds(start + r, 1), s * T : (s + 1) * T]
+                rows_ref[c, r, s : s + 1, :] = light[c, pl.ds(start + r, 1), (S - 1 - s) * T : (S - s) * T]
+
+
+def view_row(layer, h):
+    return 64 * ((VIEW_TURN - layer) & 3) + 4 * (1 - h)
 
 
 def shade_kernel(front_ref, cells_ref, ext_ref, gain_ref, slope_ref, base_ref, const_ref, send_ref, shade):
@@ -232,8 +246,8 @@
         for q in range(2):
             r = 2 * i + q
             for edge in range(2):
-                low = front_ref[i, 3, q] if edge == 0 else cells_ref[layers - 2, r]
-                high = cells_ref[1, r] if edge == 0 else front_ref[i, 4, q]
+                low = front_ref[light_slot(i), 3, q] if edge == 0 else cells_ref[layers - 2, r]
+                high = cells_ref[1, r] if edge == 0 else front_ref[light_slot(i), 4, q]
                 gx = 0.5 * (high.astype(F32) - low.astype(F32))
                 facing = (0.8 * gx + slope_ref[edge, 0, r]) * lax.rsqrt(slope_ref[edge, 1, r] + gx * gx)
                 shade[edge, r] = 0.65 + 0.35 * facing
@@ -243,7 +257,7 @@
 
     def channel(c, carry):
         scale = const_ref[ABSORB + c]
-        front = [halves(front_ref[r // 2, c, r % 2].astype(F32)) for r in range(rows)]
+        front = [halves(front_ref[light_slot(r // 2), c, r % 2].astype(F32)) for r in range(rows)]
         for layer in range(layers):
             total = list(halves(base_ref[layer, c]))
             for r in range(rows):
@@ -255,17 +269,17 @@
                     ext = halves(ext_ref[layer, r])
                     front[r] = blur(*[f * jnp.exp(scale * e) for f, e in zip(front[r], ext)])
             for h in range(2):
-                send_ref[pl.ds(layer * 64 + h * 4 + c, S, stride=8), :] = total[h]
+                send_ref[pl.ds(view_row(layer, h) + c, S, stride=8), :] = total[h]
         return carry
 
     lax.fori_loop(0, 3, channel, 0)
     for layer in range(layers):
         for h in range(2):
-            send_ref[pl.ds(layer * 64 + h * 4 + 3, S, stride=8), :] = base_ref[layer, 3, :, h * H : (h + 1) * H]
+            send_ref[pl.ds(view_row(layer, h) + 3, S, stride=8), :] = base_ref[layer, 3, :, h * H : (h + 1) * H]
 
 
 def merge_kernel(parts_ref, sign_ref, out_ref):
-    back = sign_ref[0] < 0.0
+    back = sign_ref[0] >= 0.0
 
     def over(near, far):
         through = 1.0 - near[3]
@@ -276,6 +290,8 @@
         j = jnp.where(back, 7 - i, i)
         part = [parts_ref[pl.ds(4 * j + c, 8, stride=32), :] for c in range(4)]
         held = part if held is None else over(held, part)
+    if VIEW_TURN != 3:
+        held = [pltpu.roll(x, 6 - 2 * VIEW_TURN, 0) for x in held]
     for step in (1, 2, 4):
         other = [pltpu.roll(x, 8 - step, 0) for x in held]
         near = [jnp.where(back, o, h) for o, h in zip(other, held)]
@@ -323,7 +339,9 @@
     )(*[in_hbm(x) for x in (density, *small)], view_sign)
     const = in_vmem(const)
 
-    recv = lax.all_to_all(send, "light", 0, 0)
+    light_list = [sorted(range(lights), key=light_slot)]
+    view_list = [[(16 * VIEW_TURN + 15 - k) % views for k in range(views)]]
+    recv = lax.all_to_all(send, "light", 0, 0, axis_index_groups=light_list)
 
     ext, gain, slope, base, light_rows = pl.pallas_call(
         local_kernel,
@@ -349,7 +367,7 @@
         compiler_params=LIMIT,
         name="propagate",
     )(in_vmem(recv), in_vmem(light_rows), const)
-    front = lax.all_to_all(fronts, "light", 0, 0)
+    front = lax.all_to_all(fronts, "light", 0, 0, axis_index_groups=light_list)
 
     partial = pl.pallas_call(
         shade_kernel,
@@ -361,7 +379,8 @@
         name="shade",
     )(*[in_vmem(x) for x in (front, cells, ext, gain, slope, base)], const)
 
-    parts = lax.all_to_all(partial.reshape(views, 4, H), "view", 0, 0).reshape(views * 4, H)
+    parts = lax.all_to_all(partial.reshape(views, 4, H), "view", 0, 0, axis_index_groups=view_list)
+    parts = parts.reshape(views * 4, H)
     return pl.pallas_call(
         merge_kernel,
         out_shape=jax.ShapeDtypeStruct((4, H), F32),

time: 65.9 us -> 59.3 us (0.90)
  waiting for transfers between devices: 7.42 us -> 2.26 us
  blocking collectives: 42 us -> 39.3 us
  starting transfers between devices: 7.65 us -> 8.91 us
    all_to_all x1, waiting for transfers between devices: 7.42 us -> 2.26 us  [body(): recv = lax.all_to_all(send, 'light', 0, 0, axis_index_groups=light_list)]
    all_to_all x2, blocking collectives: 42 us -> 39.3 us  [the longest x1 26.5 us: body(): lax.all_to_all(partial.reshape(views, 4, H), 'view', 0, 0, axis_index_gro...]
    all_to_all x1, starting transfers between devices: 7.65 us -> 8.91 us  [body(): recv = lax.all_to_all(send, 'light', 0, 0, axis_index_groups=light_list)]
where the time goes in v4:
time: 59.3 us; the launch traced here: 59 us
  blocking collectives  39.3 us (66%)
  starting transfers between devices  8.91 us (15%)
  Pallas kernels  7.77 us (13%)
  waiting for transfers between devices  2.26 us (4%)
  between operations  0.69 us (1%)
    all_to_all x1, blocking collectives, body(): lax.all_to_all(partial.reshape(views, 4, H), 'view', 0, 0, axis_index_gro...  26.5 us
    all_to_all x1, blocking collectives, body(): front = lax.all_to_all(fronts, 'light', 0, 0, axis_index_groups=light_list)  12.8 us
    all_to_all x1, starting transfers between devices, body(): recv = lax.all_to_all(send, 'light', 0, 0, axis_index_groups=light_list)  8.91 us
    all_to_all x1, waiting for transfers between devices, body(): recv = lax.all_to_all(send, 'light', 0, 0, axis_index_groups=light_list)  2.26 us
    pallas_call x1, Pallas kernels, body(): pl.pallas_call(propagate_kernel, out_shape=out((lights, 5, 2, S, T), BF16...  2.22 us
    pallas_call x1, Pallas kernels, body(): pl.pallas_call(local_kernel, out_shape=(out((layers, rows, S, T), F32), o...  2.01 us
    pallas_call x1, Pallas kernels, body(): pl.pallas_call(lambda *refs: prepare_kernel(*refs, total_y=rows * views),...  1.75 us
  transfers between devices with their start and end apart: 1, of which 1 were waited for; matrix products, arithmetic and copies ran while one was open for 0% of the time, Pallas kernels for 3%

profile of v4, /device:TPU:1, one launch (start us, length us, event | category | flops | bytes accessed | tf_op | source)
XLA Modules:
  0.0 59.0 jit_solution(14046846557473754470)
XLA Ops:
  0.7 1.8 %prepare.1 = (bf16[4,16,8,256]{3,2,1,0:T(8,128)(2,1)S(1)}, f32[22,8,128]{2,1,0:T(8,128)S(1)}, bf16[8,4,2,8,256]{4,3,2,1,0:T(8,128)(2,1)}) custom-call(bf16[4,16,2048]{2,1,0:T(8,128)(2,1)} %refs_0_.1, s32[1,1,16]{2,1,0:T(1,128)} %refs_1_.1, f32[4,4]{1,0:T(4,128)} %refs_2_.1, f32[3]{0:T(128)} %refs_3_.1, f32[1]{0:T(128)S(6)} %copy.7.refs_4_.sign_ref), custom_call_target="tpu_custom_call" | custom-call | tf_op jit(solution)/shard_map/prepare/pallas_call | solution.py:319
  2.4 8.9 %all-to-all-start = ((bf16[8,4,2,8,256]{4,3,2,1,0:T(8,128)(2,1)}), bf16[8,4,2,8,256]{4,3,2,1,0:T(8,128)(2,1)S(1)}, u32[]{:S(2)}, u32[]{:S(2)}) async-start(bf16[8,4,2,8,256]{4,3,2,1,0:T(8,128)(2,1)} %get-tuple-element.13), calls=%async_computation | async-start | bytes 524288 | tf_op jit(solution)/shard_map/all_to_all | solution.py:344
  11.3 2.0 %local.1 = (f32[4,16,8,256]{3,2,1,0:T(8,128)S(1)}, f32[4,16,3,8,256]{4,3,2,1,0:T(8,128)S(1)}, f32[2,2,16,8,256]{4,3,2,1,0:T(8,128)S(1)}, f32[4,4,8,256]{3,2,1,0:T(8,128)S(1)}, f32[3,2,8,256]{3,2,1,0:T(8,128)S(1)}) custom-call(bf16[4,16,8,256]{3,2,1,0:T(8,128)(2,1)S(1)} %get-tuple-element.14.cells_ref, f32[3,16,2048]{2,1,0:T(8,128)} %light_ref.1, ...), custom_call_target="tpu_custom_call" | custom-call | tf_op jit(solution)/shard_map/local/pallas_call | solution.py:346
  13.3 2.3 %all-to-all-done.recv_ref = bf16[8,4,2,8,256]{4,3,2,1,0:T(8,128)(2,1)S(1)} async-done(((bf16[8,4,2,8,256]{4,3,2,1,0:T(8,128)(2,1)}), bf16[8,4,2,8,256]{4,3,2,1,0:T(8,128)(2,1)S(1)}, u32[]{:S(2)}, u32[]{:S(2)}) %all-to-all-start) | async-done | bytes 262176 | tf_op jit(solution)/shard_map/all_to_all | solution.py:344
  15.6 2.2 %propagate.1 = bf16[8,5,2,8,256]{4,3,2,1,0:T(8,128)(2,1)S(1)} custom-call(bf16[8,4,2,8,256]{4,3,2,1,0:T(8,128)(2,1)S(1)} %all-to-all-done.recv_ref, f32[3,2,8,256]{3,2,1,0:T(8,128)S(1)} %get-tuple-element.16.rows_ref, f32[22,8,128]{2,1,0:T(8,128)S(1)} %get-tuple-element.15.const_ref), custom_call_target="tpu_custom_call" | custom-call | tf_op jit(solution)/shard_map/propagate/pallas_call | solution.py:362
  17.8 12.8 %all_to_all.15.front_ref = bf16[8,5,2,8,256]{4,3,2,1,0:T(8,128)(2,1)S(1)} all-to-all(bf16[8,5,2,8,256]{4,3,2,1,0:T(8,128)(2,1)S(1)} %propagate.1), channel_id=1, replica_groups={{320,384,448,0,64,128,192,256},{321,385,449,1,65,129,193,257},{322,386,..., dimensions={0} | all-to-all | bytes 655360 | tf_op jit(solution)/shard_map/all_to_all | solution.py:370
  30.6 1.1 %shade.1 = f32[256,128]{1,0:T(8,128)S(1)} custom-call(bf16[8,5,2,8,256]{4,3,2,1,0:T(8,128)(2,1)S(1)} %all_to_all.15.front_ref, bf16[4,16,8,256]{3,2,1,0:T(8,128)(2,1)S(1)} %get-tuple-element.14.cells_ref, f32[4,16,8,256]{3,2,1,0:T(8,128)S(1)} %get-tuple-element.17.ext_ref, f32[4,16,3,8,256]{4,3,2,1,0:T(8,128)S(1)} %get-tuple-element.18.gain_ref, ...), custom_call_target="tpu_custom_call" | custom-call | tf_op jit(solution)/shard_map/shade/pallas_call | solution.py:372
  31.7 26.5 %all_to_all.16 = f32[64,4,128]{2,1,0:T(4,128)S(1)} all-to-all(f32[64,4,128]{2,1,0:T(4,128)S(1)} %bitcast.2), channel_id=1, replica_groups={{63,62,61,60,59,58,57,56,55,54,53,52,51,50,49,48,47,46,45,44,43,42,41,4..., dimensions={0} | all-to-all | bytes 262144 | tf_op jit(solution)/shard_map/all_to_all | solution.py:382
  58.3 0.7 %merge.1 = f32[4,128]{1,0:T(4,128)} custom-call(f32[256,128]{1,0:T(8,128)S(1)} %bitcast.3, f32[1]{0:T(128)S(6)} %copy.7.refs_4_.sign_ref), custom_call_target="tpu_custom_call" | custom-call | tf_op jit(solution)/shard_map/merge/pallas_call | solution.py:384
Async XLA Ops:
  2.4 13.2 %all-to-all-start = ((bf16[8,4,2,8,256]{4,3,2,1,0:T(8,128)(2,1)}), bf16[8,4,2,8,256]{4,3,2,1,0:T(8,128)(2,1)S(1)}, u32[]{:S(2)}, u32[]{:S(2)}) async-start(bf16[8,4,2,8,256]{4,3,2,1,0:T(8,128)(2,1)} %get-tuple-element.13), calls=%async_computation | async-start | bytes 524288 | tf_op jit(solution)/shard_map/all_to_all | solution.py:344

commit v5 on v4

--- a/solution.py
+++ b/solution.py
@@ -70,9 +70,6 @@
             occ = jnp.where(sub == s, occ_ref[0, 0, 2 * (S - 1 - s) + h].astype(F32), occ)
         out.append(occ)
     return out
-
-
-TINY = 2.0**-100
 
 
 def prepare_kernel(
@@ -102,7 +99,7 @@
                 tmp[layer, h, pl.ds(s, rows, stride=S), :] = x[:, column : column + H]
         y = jnp.concatenate([tmp[layer, h].reshape(rows, S, H) for h in range(2)], axis=2)
         cells_ref[layer] = y.astype(BF16)
-        sent = jnp.where(mask, y, -jnp.maximum(y, TINY)).astype(BF16)
+        sent = jnp.where(mask, y, -1.0).astype(BF16)
         for k in range(rows // 2):
             packed[light_slot(k), layer] = sent[2 * k : 2 * k + 2]
         stores[layer].start()
@@ -120,18 +117,10 @@
         store.wait()
 
 
-def propagate_kernel(recv_ref, rows_ref, const_ref, send_ref):
+def propagate_kernel(recv_ref, rows_ref, const_ref, low_ref, high_ref, send_ref):
+    del low_ref, high_ref
     blocks, layers = recv_ref.shape[0], recv_ref.shape[1]
     scale = [const_ref[ABSORB + c] for c in range(3)]
-
-    def density(slot, layer):
-        d = recv_ref[slot, layer].astype(F32)
-        return jnp.where(d >= 0.0, d, jnp.where(d > -2.0 * TINY, 0.0, -d)).astype(BF16)
-
-    for k in range(blocks):
-        slot, none = light_slot(k), jnp.zeros((2, S, T), BF16)
-        send_ref[slot, 3] = density(light_slot(k - 1), layers - 1) if k > 0 else none
-        send_ref[slot, 4] = density(light_slot(k + 1), 0) if k < blocks - 1 else none
 
     def extinction(k):
         out = []
@@ -239,15 +228,14 @@
     return 64 * ((VIEW_TURN - layer) & 3) + 4 * (1 - h)
 
 
-def shade_kernel(front_ref, cells_ref, ext_ref, gain_ref, slope_ref, base_ref, const_ref, send_ref, shade):
+def shade_kernel(front_ref, low_ref, high_ref, cells_ref, ext_ref, gain_ref, slope_ref, base_ref, const_ref, send_ref, shade):
     layers, rows = ext_ref.shape[0], ext_ref.shape[1]
 
     def finish(i, carry):
-        for q in range(2):
-            r = 2 * i + q
+        for r in (2 * i, 2 * i + 1):
             for edge in range(2):
-                low = front_ref[light_slot(i), 3, q] if edge == 0 else cells_ref[layers - 2, r]
-                high = cells_ref[1, r] if edge == 0 else front_ref[light_slot(i), 4, q]
+                low = low_ref[r] if edge == 0 else cells_ref[layers - 2, r]
+                high = cells_ref[1, r] if edge == 0 else high_ref[r]
                 gx = 0.5 * (high.astype(F32) - low.astype(F32))
                 facing = (0.8 * gx + slope_ref[edge, 0, r]) * lax.rsqrt(slope_ref[edge, 1, r] + gx * gx)
                 shade[edge, r] = 0.65 + 0.35 * facing
@@ -341,6 +329,10 @@
 
     light_list = [sorted(range(lights), key=light_slot)]
     view_list = [[(16 * VIEW_TURN + 15 - k) % views for k in range(views)]]
+    ends = lights - 1
+    first, last = cells[0], cells[layers - 1]
+    low = lax.ppermute(last, "light", [(i, i + 1) for i in range(ends)])
+    high = lax.ppermute(first, "light", [(i + 1, i) for i in range(ends)])
     recv = lax.all_to_all(send, "light", 0, 0, axis_index_groups=light_list)
 
     ext, gain, slope, base, light_rows = pl.pallas_call(
@@ -361,23 +353,23 @@
 
     fronts = pl.pallas_call(
         propagate_kernel,
-        out_shape=out((lights, 5, 2, S, T), BF16),
-        in_specs=[VMEM, VMEM, VMEM],
+        out_shape=out((lights, 3, 2, S, T), BF16),
+        in_specs=[VMEM] * 5,
         out_specs=VMEM,
         compiler_params=LIMIT,
         name="propagate",
-    )(in_vmem(recv), in_vmem(light_rows), const)
+    )(in_vmem(recv), in_vmem(light_rows), const, in_vmem(low), in_vmem(high))
     front = lax.all_to_all(fronts, "light", 0, 0, axis_index_groups=light_list)
 
     partial = pl.pallas_call(
         shade_kernel,
         out_shape=out((views * 4, H), F32),
-        in_specs=[VMEM] * 7,
+        in_specs=[VMEM] * 9,
         out_specs=VMEM,
         scratch_shapes=[pltpu.VMEM((2, rows, S, T), F32)],
         compiler_params=LIMIT,
         name="shade",
-    )(*[in_vmem(x) for x in (front, cells, ext, gain, slope, base)], const)
+    )(*[in_vmem(x) for x in (front, low, high, cells, ext, gain, slope, base)], const)
 
     parts = lax.all_to_all(partial.reshape(views, 4, H), "view", 0, 0, axis_index_groups=view_list)
     parts = parts.reshape(views * 4, H)

time: 59.3 us -> 58.2 us (0.981)
  starting transfers between devices: 8.91 us -> 14.2 us
  blocking collectives: 39.3 us -> 34.8 us
  waiting for transfers between devices: 2.26 us -> 0.37 us
    ppermute x0 -> x2, starting transfers between devices: none -> 5.28 us  [the longest x1 3.99 us: body(): low = lax.ppermute(last, 'light', [(i, i + 1) for i in range(ends)])]
    all_to_all x1, blocking collectives: 26.5 us -> 22.6 us  [body(): lax.all_to_all(partial.reshape(views, 4, H), 'view', 0, 0, axis_index_gro...]
    all_to_all x1, waiting for transfers between devices: 2.26 us -> 0.01 us  [body(): recv = lax.all_to_all(send, 'light', 0, 0, axis_index_groups=light_list)]
  transfers between devices with their start and end apart: 1 -> 3, of which waited for: 1 -> 1; matrix products, arithmetic and copies ran while one was open for 0% -> 0% of each run, Pallas kernels for 3% -> 3%
where the time goes in v5:
time: 58.2 us; the launch traced here: 57.8 us
  blocking collectives  34.8 us (60%)
  starting transfers between devices  14.2 us (24%)
  Pallas kernels  7.73 us (13%)
  between operations  0.71 us (1%)
    all_to_all x1, blocking collectives, body(): lax.all_to_all(partial.reshape(views, 4, H), 'view', 0, 0, axis_index_gro...  22.6 us
    all_to_all x1, blocking collectives, body(): front = lax.all_to_all(fronts, 'light', 0, 0, axis_index_groups=light_list)  12.2 us
    all_to_all x1, starting transfers between devices, body(): recv = lax.all_to_all(send, 'light', 0, 0, axis_index_groups=light_list)  8.91 us
    ppermute x1, starting transfers between devices, body(): low = lax.ppermute(last, 'light', [(i, i + 1) for i in range(ends)])  3.99 us
    pallas_call x1, Pallas kernels, body(): pl.pallas_call(propagate_kernel, out_shape=out((lights, 3, 2, S, T), BF16...  2.18 us
    pallas_call x1, Pallas kernels, body(): pl.pallas_call(local_kernel, out_shape=(out((layers, rows, S, T), F32), o...  2.02 us
    pallas_call x1, Pallas kernels, body(): pl.pallas_call(lambda *refs: prepare_kernel(*refs, total_y=rows * views),...  1.74 us
    ppermute x1, starting transfers between devices, body(): high = lax.ppermute(first, 'light', [(i + 1, i) for i in range(ends)])  1.29 us
  transfers between devices with their start and end apart: 3, of which 1 were waited for; matrix products, arithmetic and copies ran while one was open for 0% of the time, Pallas kernels for 3%

profile of v5, /device:TPU:1, one launch (start us, length us, event | category | flops | bytes accessed | tf_op | source)
XLA Modules:
  0.0 57.8 jit_solution(13993220491427268059)
XLA Ops:
  0.7 1.7 %prepare.1 = (bf16[4,16,8,256]{3,2,1,0:T(8,128)(2,1)S(1)}, f32[22,8,128]{2,1,0:T(8,128)S(1)}, bf16[8,4,2,8,256]{4,3,2,1,0:T(8,128)(2,1)}) custom-call(bf16[4,16,2048]{2,1,0:T(8,128)(2,1)} %refs_0_.1, s32[1,1,16]{2,1,0:T(1,128)} %refs_1_.1, f32[4,4]{1,0:T(4,128)} %refs_2_.1, f32[3]{0:T(128)} %refs_3_.1, f32[1]{0:T(128)S(6)} %copy.7.refs_4_.sign_ref), custom_call_target="tpu_custom_call" | custom-call | tf_op jit(solution)/shard_map/prepare/pallas_call | solution.py:307
  2.4 8.9 %all-to-all-start = ((bf16[8,4,2,8,256]{4,3,2,1,0:T(8,128)(2,1)}), bf16[8,4,2,8,256]{4,3,2,1,0:T(8,128)(2,1)S(1)}, u32[]{:S(2)}, u32[]{:S(2)}) async-start(bf16[8,4,2,8,256]{4,3,2,1,0:T(8,128)(2,1)} %get-tuple-element.13), calls=%async_computation | async-start | bytes 524288 | tf_op jit(solution)/shard_map/all_to_all | solution.py:336
  11.3 1.3 %collective-permute-start.1 = (bf16[16,8,256]{2,1,0:T(8,128)(2,1)S(1)}, bf16[16,8,256]{2,1,0:T(8,128)(2,1)S(1)}, u32[]{:S(2)}, u32[]{:S(2)}) collective-permute-start(bf16[16,8,256]{2,1,0:T(8,128)(2,1)S(1)} %get-tuple-element.21), channel_id=1, source_target_pairs={{64,0},{128,64},{192,128},{256,192},{320,256},{384,320},{448,384},... | collective-permute-start | bytes 196616 | tf_op jit(solution)/shard_map/ppermute | solution.py:335
  12.6 4.0 %collective-permute-start = (bf16[16,8,256]{2,1,0:T(8,128)(2,1)S(1)}, bf16[16,8,256]{2,1,0:T(8,128)(2,1)S(1)}, u32[]{:S(2)}, u32[]{:S(2)}) collective-permute-start(bf16[16,8,256]{2,1,0:T(8,128)(2,1)S(1)} %get-tuple-element.22), channel_id=1, source_target_pairs={{0,64},{64,128},{128,192},{192,256},{256,320},{320,384},{384,448},... | collective-permute-start | bytes 196616 | tf_op jit(solution)/shard_map/ppermute | solution.py:334
  16.6 2.0 %local.1 = (f32[4,16,8,256]{3,2,1,0:T(8,128)S(1)}, f32[4,16,3,8,256]{4,3,2,1,0:T(8,128)S(1)}, f32[2,2,16,8,256]{4,3,2,1,0:T(8,128)S(1)}, f32[4,4,8,256]{3,2,1,0:T(8,128)S(1)}, f32[3,2,8,256]{3,2,1,0:T(8,128)S(1)}) custom-call(bf16[4,16,8,256]{3,2,1,0:T(8,128)(2,1)S(1)} %get-tuple-element.14.cells_ref, f32[3,16,2048]{2,1,0:T(8,128)} %light_ref.1, ...), custom_call_target="tpu_custom_call" | custom-call | tf_op jit(solution)/shard_map/local/pallas_call | solution.py:338
  18.6 0.0 collective-permute-done.1.high_ref
  18.7 0.4 collective-permute-done.low_ref
  19.0 0.0 all-to-all-done.recv_ref
  19.0 2.2 %propagate.1 = bf16[8,3,2,8,256]{4,3,2,1,0:T(8,128)(2,1)S(1)} custom-call(bf16[8,4,2,8,256]{4,3,2,1,0:T(8,128)(2,1)S(1)} %all-to-all-done.recv_ref, f32[3,2,8,256]{3,2,1,0:T(8,128)S(1)} %get-tuple-element.16.rows_ref, f32[22,8,128]{2,1,0:T(8,128)S(1)} %get-tuple-element.15.const_ref, bf16[16,8,256]{2,1,0:T(8,128)(2,1)S(1)} %collective-permute-done.low_ref, ...), custom_call_target="tpu_custom_call" | custom-call | tf_op jit(solution)/shard_map/propagate/pallas_call | solution.py:354
  21.2 12.2 %all_to_all.15.front_ref = bf16[8,3,2,8,256]{4,3,2,1,0:T(8,128)(2,1)S(1)} all-to-all(bf16[8,3,2,8,256]{4,3,2,1,0:T(8,128)(2,1)S(1)} %propagate.1), channel_id=1, replica_groups={{320,384,448,0,64,128,192,256},{321,385,449,1,65,129,193,257},{322,386,..., dimensions={0} | all-to-all | bytes 393216 | tf_op jit(solution)/shard_map/all_to_all | solution.py:362
  33.4 1.1 %shade.1 = f32[256,128]{1,0:T(8,128)S(1)} custom-call(bf16[8,3,2,8,256]{4,3,2,1,0:T(8,128)(2,1)S(1)} %all_to_all.15.front_ref, bf16[16,8,256]{2,1,0:T(8,128)(2,1)S(1)} %collective-permute-done.low_ref, bf16[16,8,256]{2,1,0:T(8,128)(2,1)S(1)} %collective-permute-done.1.high_ref, bf16[4,16,8,256]{3,2,1,0:T(8,128)(2,1)S(1)} %get-tuple-element.14.cells_ref, ...), custom_call_target="tpu_custom_call" | custom-call | tf_op jit(solution)/shard_map/shade/pallas_call | solution.py:364
  34.6 22.6 %all_to_all.16 = f32[64,4,128]{2,1,0:T(4,128)S(1)} all-to-all(f32[64,4,128]{2,1,0:T(4,128)S(1)} %bitcast.6), channel_id=1, replica_groups={{63,62,61,60,59,58,57,56,55,54,53,52,51,50,49,48,47,46,45,44,43,42,41,4..., dimensions={0} | all-to-all | bytes 262144 | tf_op jit(solution)/shard_map/all_to_all | solution.py:374
  57.1 0.7 %merge.1 = f32[4,128]{1,0:T(4,128)} custom-call(f32[256,128]{1,0:T(8,128)S(1)} %bitcast.7, f32[1]{0:T(128)S(6)} %copy.7.refs_4_.sign_ref), custom_call_target="tpu_custom_call" | custom-call | tf_op jit(solution)/shard_map/merge/pallas_call | solution.py:376
  (1 shorter events, 0.0 us)
Async XLA Ops:
  2.4 16.6 %all-to-all-start = ((bf16[8,4,2,8,256]{4,3,2,1,0:T(8,128)(2,1)}), bf16[8,4,2,8,256]{4,3,2,1,0:T(8,128)(2,1)S(1)}, u32[]{:S(2)}, u32[]{:S(2)}) async-start(bf16[8,4,2,8,256]{4,3,2,1,0:T(8,128)(2,1)} %get-tuple-element.13), calls=%async_computation | async-start | bytes 524288 | tf_op jit(solution)/shard_map/all_to_all | solution.py:336
  11.3 7.3 %collective-permute-start.1 = (bf16[16,8,256]{2,1,0:T(8,128)(2,1)S(1)}, bf16[16,8,256]{2,1,0:T(8,128)(2,1)S(1)}, u32[]{:S(2)}, u32[]{:S(2)}) collective-permute-start(bf16[16,8,256]{2,1,0:T(8,128)(2,1)S(1)} %get-tuple-element.21), channel_id=1, source_target_pairs={{64,0},{128,64},{192,128},{256,192},{320,256},{384,320},{448,384},... | collective-permute-start | bytes 196616 | tf_op jit(solution)/shard_map/ppermute | solution.py:335
  12.6 6.4 %collective-permute-start = (bf16[16,8,256]{2,1,0:T(8,128)(2,1)S(1)}, bf16[16,8,256]{2,1,0:T(8,128)(2,1)S(1)}, u32[]{:S(2)}, u32[]{:S(2)}) collective-permute-start(bf16[16,8,256]{2,1,0:T(8,128)(2,1)S(1)} %get-tuple-element.22), channel_id=1, source_target_pairs={{0,64},{64,128},{128,192},{192,256},{256,320},{320,384},{384,448},... | collective-permute-start | bytes 196616 | tf_op jit(solution)/shard_map/ppermute | solution.py:334

commit v6 on v5

--- a/solution.py
+++ b/solution.py
@@ -16,12 +16,13 @@
 SMEM = pl.BlockSpec(memory_space=pltpu.SMEM)
 
 
-LIGHT_FIRST, LIGHT_STEP = 5, 1
-VIEW_TURN = 3
-
-
-def light_slot(k):
-    return (LIGHT_STEP * (k - LIGHT_FIRST)) & 7
+CELLS_FIRST = 6
+FRONT_FIRST = 4
+VIEW_FIRST = 61
+
+
+def light_slot(k, first):
+    return (k - first) & 7
 
 
 def halves(x):
@@ -101,7 +102,7 @@
         cells_ref[layer] = y.astype(BF16)
         sent = jnp.where(mask, y, -1.0).astype(BF16)
         for k in range(rows // 2):
-            packed[light_slot(k), layer] = sent[2 * k : 2 * k + 2]
+            packed[light_slot(k, CELLS_FIRST), layer] = sent[2 * k : 2 * k + 2]
         stores[layer].start()
     for copy in small[1:]:
         copy.wait()
@@ -125,14 +126,14 @@
     def extinction(k):
         out = []
         for layer in range(layers):
-            for d in halves(recv_ref[light_slot(k), layer].astype(F32)):
+            for d in halves(recv_ref[light_slot(k, CELLS_FIRST), layer].astype(F32)):
                 out.append(jnp.where(d < 0.0, 0.0, softplus(polynomial(const_ref, 0, d))))
         return tuple(out)
 
     def emit(k, front):
         for c in range(3):
-            send_ref[light_slot(k), c, :, :, :H] = front[2 * c].astype(BF16)
-            send_ref[light_slot(k), c, :, :, H:] = front[2 * c + 1].astype(BF16)
+            send_ref[light_slot(k, FRONT_FIRST), c, :, :, :H] = front[2 * c].astype(BF16)
+            send_ref[light_slot(k, FRONT_FIRST), c, :, :, H:] = front[2 * c + 1].astype(BF16)
 
     def block(k, carry):
         front, ext = list(carry[0]), carry[1]
@@ -224,8 +225,12 @@
                 rows_ref[c, r, s : s + 1, :] = light[c, pl.ds(start + r, 1), (S - 1 - s) * T : (S - s) * T]
 
 
-def view_row(layer, h):
-    return 64 * ((VIEW_TURN - layer) & 3) + 4 * (1 - h)
+def place(send_ref, layer, h, c, value):
+    start = (VIEW_FIRST - 16 * layer - h - 14) % 64
+    split = min(S, (65 - start) // 2)
+    send_ref[pl.ds(4 * start + c, split, stride=8), :] = value[:split]
+    if split < S:
+        send_ref[pl.ds(4 * (start + 2 * split - 64) + c, S - split, stride=8), :] = value[split:]
 
 
 def shade_kernel(front_ref, low_ref, high_ref, cells_ref, ext_ref, gain_ref, slope_ref, base_ref, const_ref, send_ref, shade):
@@ -245,7 +250,7 @@
 
     def channel(c, carry):
         scale = const_ref[ABSORB + c]
-        front = [halves(front_ref[light_slot(r // 2), c, r % 2].astype(F32)) for r in range(rows)]
+        front = [halves(front_ref[light_slot(r // 2, FRONT_FIRST), c, r % 2].astype(F32)) for r in range(rows)]
         for layer in range(layers):
             total = list(halves(base_ref[layer, c]))
             for r in range(rows):
@@ -257,17 +262,18 @@
                     ext = halves(ext_ref[layer, r])
                     front[r] = blur(*[f * jnp.exp(scale * e) for f, e in zip(front[r], ext)])
             for h in range(2):
-                send_ref[pl.ds(view_row(layer, h) + c, S, stride=8), :] = total[h]
+                place(send_ref, layer, h, c, total[h])
         return carry
 
     lax.fori_loop(0, 3, channel, 0)
     for layer in range(layers):
         for h in range(2):
-            send_ref[pl.ds(view_row(layer, h) + 3, S, stride=8), :] = base_ref[layer, 3, :, h * H : (h + 1) * H]
+            place(send_ref, layer, h, 3, base_ref[layer, 3, :, h * H : (h + 1) * H])
 
 
 def merge_kernel(parts_ref, sign_ref, out_ref):
     back = sign_ref[0] >= 0.0
+    late = 63 - VIEW_FIRST
 
     def over(near, far):
         through = 1.0 - near[3]
@@ -276,10 +282,10 @@
     held = None
     for i in range(8):
         j = jnp.where(back, 7 - i, i)
-        part = [parts_ref[pl.ds(4 * j + c, 8, stride=32), :] for c in range(4)]
+        part = [parts_ref[pl.ds(4 * ((j - late) & 7) + c, 8, stride=32), :] for c in range(4)]
+        if min(i, 7 - i) < late:
+            part = [jnp.where(j < late, pltpu.roll(x, 1, 0), x) for x in part]
         held = part if held is None else over(held, part)
-    if VIEW_TURN != 3:
-        held = [pltpu.roll(x, 6 - 2 * VIEW_TURN, 0) for x in held]
     for step in (1, 2, 4):
         other = [pltpu.roll(x, 8 - step, 0) for x in held]
         near = [jnp.where(back, o, h) for o, h in zip(other, held)]
@@ -327,13 +333,15 @@
     )(*[in_hbm(x) for x in (density, *small)], view_sign)
     const = in_vmem(const)
 
-    light_list = [sorted(range(lights), key=light_slot)]
-    view_list = [[(16 * VIEW_TURN + 15 - k) % views for k in range(views)]]
+    cells_list, front_list = [
+        [sorted(range(lights), key=lambda k: light_slot(k, first))] for first in (CELLS_FIRST, FRONT_FIRST)
+    ]
+    view_list = [[(VIEW_FIRST - k) % views for k in range(views)]]
     ends = lights - 1
     first, last = cells[0], cells[layers - 1]
     low = lax.ppermute(last, "light", [(i, i + 1) for i in range(ends)])
     high = lax.ppermute(first, "light", [(i + 1, i) for i in range(ends)])
-    recv = lax.all_to_all(send, "light", 0, 0, axis_index_groups=light_list)
+    recv = lax.all_to_all(send, "light", 0, 0, axis_index_groups=cells_list)
 
     ext, gain, slope, base, light_rows = pl.pallas_call(
         local_kernel,
@@ -359,7 +367,7 @@
         compiler_params=LIMIT,
         name="propagate",
     )(in_vmem(recv), in_vmem(light_rows), const, in_vmem(low), in_vmem(high))
-    front = lax.all_to_all(fronts, "light", 0, 0, axis_index_groups=light_list)
+    front = lax.all_to_all(fronts, "light", 0, 0, axis_index_groups=front_list)
 
     partial = pl.pallas_call(
         shade_kernel,

time: 58.2 us -> 57.2 us (0.983)
  starting transfers between devices: 14.2 us -> 13.4 us
    all_to_all x1, starting transfers between devices: 8.91 us -> 8.12 us  [body(): recv = lax.all_to_all(send, 'light', 0, 0, axis_index_groups=cells_list)]
    all_to_all x1, blocking collectives: 12.2 us -> 11.5 us  [body(): front = lax.all_to_all(fronts, 'light', 0, 0, axis_index_groups=front_list)]
  transfers between devices with their start and end apart: 3 -> 3, of which waited for: 1 -> 1; matrix products, arithmetic and copies ran while one was open for 0% -> 0% of each run, Pallas kernels for 3% -> 4%
where the time goes in v6:
time: 57.2 us; the launch traced here: 56.9 us
  blocking collectives  34.6 us (60%)
  starting transfers between devices  13.4 us (23%)
  Pallas kernels  7.74 us (14%)
  between operations  0.71 us (1%)
    all_to_all x1, blocking collectives, body(): lax.all_to_all(partial.reshape(views, 4, H), 'view', 0, 0, axis_index_gro...  23.1 us
    all_to_all x1, blocking collectives, body(): front = lax.all_to_all(fronts, 'light', 0, 0, axis_index_groups=front_list)  11.5 us
    all_to_all x1, starting transfers between devices, body(): recv = lax.all_to_all(send, 'light', 0, 0, axis_index_groups=cells_list)  8.12 us
    ppermute x1, starting transfers between devices, body(): low = lax.ppermute(last, 'light', [(i, i + 1) for i in range(ends)])  3.99 us
    pallas_call x1, Pallas kernels, body(): pl.pallas_call(propagate_kernel, out_shape=out((lights, 3, 2, S, T), BF16...  2.18 us
    pallas_call x1, Pallas kernels, body(): pl.pallas_call(local_kernel, out_shape=(out((layers, rows, S, T), F32), o...  2.02 us
    pallas_call x1, Pallas kernels, body(): pl.pallas_call(lambda *refs: prepare_kernel(*refs, total_y=rows * views),...  1.74 us
    ppermute x1, starting transfers between devices, body(): high = lax.ppermute(first, 'light', [(i + 1, i) for i in range(ends)])  1.29 us
  transfers between devices with their start and end apart: 3, of which 1 were waited for; matrix products, arithmetic and copies ran while one was open for 0% of the time, Pallas kernels for 4%

profile of v6, /device:TPU:1, one launch (start us, length us, event | category | flops | bytes accessed | tf_op | source)
XLA Modules:
  0.0 56.9 jit_solution(6677211403566609975)
XLA Ops:
  0.7 1.7 %prepare.1 = (bf16[4,16,8,256]{3,2,1,0:T(8,128)(2,1)S(1)}, f32[22,8,128]{2,1,0:T(8,128)S(1)}, bf16[8,4,2,8,256]{4,3,2,1,0:T(8,128)(2,1)}) custom-call(bf16[4,16,2048]{2,1,0:T(8,128)(2,1)} %refs_0_.1, s32[1,1,16]{2,1,0:T(1,128)} %refs_1_.1, f32[4,4]{1,0:T(4,128)} %refs_2_.1, f32[3]{0:T(128)} %refs_3_.1, f32[1]{0:T(128)S(6)} %copy.7.refs_4_.sign_ref), custom_call_target="tpu_custom_call" | custom-call | tf_op jit(solution)/shard_map/prepare/pallas_call | solution.py:313
  2.4 8.1 %all-to-all-start = ((bf16[8,4,2,8,256]{4,3,2,1,0:T(8,128)(2,1)}), bf16[8,4,2,8,256]{4,3,2,1,0:T(8,128)(2,1)S(1)}, u32[]{:S(2)}, u32[]{:S(2)}) async-start(bf16[8,4,2,8,256]{4,3,2,1,0:T(8,128)(2,1)} %get-tuple-element.13), calls=%async_computation | async-start | bytes 524288 | tf_op jit(solution)/shard_map/all_to_all | solution.py:344
  10.5 1.3 %collective-permute-start.1 = (bf16[16,8,256]{2,1,0:T(8,128)(2,1)S(1)}, bf16[16,8,256]{2,1,0:T(8,128)(2,1)S(1)}, u32[]{:S(2)}, u32[]{:S(2)}) collective-permute-start(bf16[16,8,256]{2,1,0:T(8,128)(2,1)S(1)} %get-tuple-element.21), channel_id=1, source_target_pairs={{64,0},{128,64},{192,128},{256,192},{320,256},{384,320},{448,384},... | collective-permute-start | bytes 196616 | tf_op jit(solution)/shard_map/ppermute | solution.py:343
  11.8 4.0 %collective-permute-start = (bf16[16,8,256]{2,1,0:T(8,128)(2,1)S(1)}, bf16[16,8,256]{2,1,0:T(8,128)(2,1)S(1)}, u32[]{:S(2)}, u32[]{:S(2)}) collective-permute-start(bf16[16,8,256]{2,1,0:T(8,128)(2,1)S(1)} %get-tuple-element.22), channel_id=1, source_target_pairs={{0,64},{64,128},{128,192},{192,256},{256,320},{320,384},{384,448},... | collective-permute-start | bytes 196616 | tf_op jit(solution)/shard_map/ppermute | solution.py:342
  15.8 2.0 %local.1 = (f32[4,16,8,256]{3,2,1,0:T(8,128)S(1)}, f32[4,16,3,8,256]{4,3,2,1,0:T(8,128)S(1)}, f32[2,2,16,8,256]{4,3,2,1,0:T(8,128)S(1)}, f32[4,4,8,256]{3,2,1,0:T(8,128)S(1)}, f32[3,2,8,256]{3,2,1,0:T(8,128)S(1)}) custom-call(bf16[4,16,8,256]{3,2,1,0:T(8,128)(2,1)S(1)} %get-tuple-element.14.cells_ref, f32[3,16,2048]{2,1,0:T(8,128)} %light_ref.1, ...), custom_call_target="tpu_custom_call" | custom-call | tf_op jit(solution)/shard_map/local/pallas_call | solution.py:346
  17.9 0.0 collective-permute-done.1.high_ref
  17.9 0.4 collective-permute-done.low_ref
  18.2 0.0 all-to-all-done.recv_ref
  18.3 2.2 %propagate.1 = bf16[8,3,2,8,256]{4,3,2,1,0:T(8,128)(2,1)S(1)} custom-call(bf16[8,4,2,8,256]{4,3,2,1,0:T(8,128)(2,1)S(1)} %all-to-all-done.recv_ref, f32[3,2,8,256]{3,2,1,0:T(8,128)S(1)} %get-tuple-element.16.rows_ref, f32[22,8,128]{2,1,0:T(8,128)S(1)} %get-tuple-element.15.const_ref, bf16[16,8,256]{2,1,0:T(8,128)(2,1)S(1)} %collective-permute-done.low_ref, ...), custom_call_target="tpu_custom_call" | custom-call | tf_op jit(solution)/shard_map/propagate/pallas_call | solution.py:362
  20.4 11.5 %all_to_all.15.front_ref = bf16[8,3,2,8,256]{4,3,2,1,0:T(8,128)(2,1)S(1)} all-to-all(bf16[8,3,2,8,256]{4,3,2,1,0:T(8,128)(2,1)S(1)} %propagate.1), channel_id=1, replica_groups={{256,320,384,448,0,64,128,192},{257,321,385,449,1,65,129,193},{258,322,..., dimensions={0} | all-to-all | bytes 393216 | tf_op jit(solution)/shard_map/all_to_all | solution.py:370
  31.9 1.1 %shade.1 = f32[256,128]{1,0:T(8,128)S(1)} custom-call(bf16[8,3,2,8,256]{4,3,2,1,0:T(8,128)(2,1)S(1)} %all_to_all.15.front_ref, bf16[16,8,256]{2,1,0:T(8,128)(2,1)S(1)} %collective-permute-done.low_ref, bf16[16,8,256]{2,1,0:T(8,128)(2,1)S(1)} %collective-permute-done.1.high_ref, bf16[4,16,8,256]{3,2,1,0:T(8,128)(2,1)S(1)} %get-tuple-element.14.cells_ref, ...), custom_call_target="tpu_custom_call" | custom-call | tf_op jit(solution)/shard_map/shade/pallas_call | solution.py:372
  33.0 23.1 %all_to_all.16 = f32[64,4,128]{2,1,0:T(4,128)S(1)} all-to-all(f32[64,4,128]{2,1,0:T(4,128)S(1)} %bitcast.6), channel_id=1, replica_groups={{61,60,59,58,57,56,55,54,53,52,51,50,49,48,47,46,45,44,43,42,41,40,39,3..., dimensions={0} | all-to-all | bytes 262144 | tf_op jit(solution)/shard_map/all_to_all | solution.py:382
  56.2 0.7 %merge.1 = f32[4,128]{1,0:T(4,128)} custom-call(f32[256,128]{1,0:T(8,128)S(1)} %bitcast.7, f32[1]{0:T(128)S(6)} %copy.7.refs_4_.sign_ref), custom_call_target="tpu_custom_call" | custom-call | tf_op jit(solution)/shard_map/merge/pallas_call | solution.py:384
  (1 shorter events, 0.0 us)
Async XLA Ops:
  2.4 15.9 %all-to-all-start = ((bf16[8,4,2,8,256]{4,3,2,1,0:T(8,128)(2,1)}), bf16[8,4,2,8,256]{4,3,2,1,0:T(8,128)(2,1)S(1)}, u32[]{:S(2)}, u32[]{:S(2)}) async-start(bf16[8,4,2,8,256]{4,3,2,1,0:T(8,128)(2,1)} %get-tuple-element.13), calls=%async_computation | async-start | bytes 524288 | tf_op jit(solution)/shard_map/all_to_all | solution.py:344
  10.5 7.3 %collective-permute-start.1 = (bf16[16,8,256]{2,1,0:T(8,128)(2,1)S(1)}, bf16[16,8,256]{2,1,0:T(8,128)(2,1)S(1)}, u32[]{:S(2)}, u32[]{:S(2)}) collective-permute-start(bf16[16,8,256]{2,1,0:T(8,128)(2,1)S(1)} %get-tuple-element.21), channel_id=1, source_target_pairs={{64,0},{128,64},{192,128},{256,192},{320,256},{384,320},{448,384},... | collective-permute-start | bytes 196616 | tf_op jit(solution)/shard_map/ppermute | solution.py:343
  11.8 6.4 %collective-permute-start = (bf16[16,8,256]{2,1,0:T(8,128)(2,1)S(1)}, bf16[16,8,256]{2,1,0:T(8,128)(2,1)S(1)}, u32[]{:S(2)}, u32[]{:S(2)}) collective-permute-start(bf16[16,8,256]{2,1,0:T(8,128)(2,1)S(1)} %get-tuple-element.22), channel_id=1, source_target_pairs={{0,64},{64,128},{128,192},{192,256},{256,320},{320,384},{384,448},... | collective-permute-start | bytes 196616 | tf_op jit(solution)/shard_map/ppermute | solution.py:342

commit v7 on v6

--- a/solution.py
+++ b/solution.py
@@ -4,6 +4,7 @@
 from jax.experimental import pallas as pl
 from jax.experimental.pallas import tpu as pltpu
 from jax.sharding import PartitionSpec as P
+
 
 S = 8
 T = 256
@@ -118,8 +119,7 @@
         store.wait()
 
 
-def propagate_kernel(recv_ref, rows_ref, const_ref, low_ref, high_ref, send_ref):
-    del low_ref, high_ref
+def propagate_kernel(recv_ref, rows_ref, const_ref, send_ref):
     blocks, layers = recv_ref.shape[0], recv_ref.shape[1]
     scale = [const_ref[ABSORB + c] for c in range(3)]
 
@@ -359,14 +359,16 @@
         name="local",
     )(in_vmem(cells), in_hbm(light_in), const, view_sign)
 
-    fronts = pl.pallas_call(
+    propagate = pl.pallas_call(
         propagate_kernel,
         out_shape=out((lights, 3, 2, S, T), BF16),
-        in_specs=[VMEM] * 5,
+        in_specs=[VMEM] * 3,
         out_specs=VMEM,
         compiler_params=LIMIT,
         name="propagate",
-    )(in_vmem(recv), in_vmem(light_rows), const, in_vmem(low), in_vmem(high))
+    )
+    fronts = propagate(in_vmem(recv), in_vmem(light_rows), const)
+    fronts, low, high = lax.optimization_barrier((fronts, low, high))
     front = lax.all_to_all(fronts, "light", 0, 0, axis_index_groups=front_list)
 
     partial = pl.pallas_call(

time: 57.2 us -> 56.6 us (0.990)
  starting transfers between devices: 13.4 us -> 12.5 us
  blocking collectives: 34.6 us -> 33.9 us
  local copies, waits for them, and re-layouts: 0.01 us -> 0.66 us
    all_to_all x1, blocking collectives: 11.5 us -> 10.4 us  [body(): front = lax.all_to_all(fronts, 'light', 0, 0, axis_index_groups=front_list)]
    ppermute x1, starting transfers between devices: 3.99 us -> 3.08 us  [body(): low = lax.ppermute(last, 'light', [(i, i + 1) for i in range(ends)])]
    ppermute x1, waiting for transfers between devices: 0.01 us -> 0.71 us  [body(): high = lax.ppermute(first, 'light', [(i + 1, i) for i in range(ends)])]
    squeeze x1, local copies, waits for them, and re-layouts: 0.01 us -> 0.66 us  [body(): first, last = (cells[0], cells[layers - 1])]
  transfers between devices with their start and end apart: 3 -> 3, of which waited for: 1 -> 1; matrix products, arithmetic and copies ran while one was open for 0% -> 1% of each run, Pallas kernels for 4% -> 7%
where the time goes in v7:
time: 56.6 us; the launch traced here: 56.2 us
  blocking collectives  33.9 us (60%)
  starting transfers between devices  12.5 us (22%)
  Pallas kernels  7.74 us (14%)
  between operations  0.72 us (1%)
  waiting for transfers between devices  0.71 us (1%)
  local copies, waits for them, and re-layouts  0.66 us (1%)
    all_to_all x1, blocking collectives, body(): lax.all_to_all(partial.reshape(views, 4, H), 'view', 0, 0, axis_index_gro...  23.5 us
    all_to_all x1, blocking collectives, body(): front = lax.all_to_all(fronts, 'light', 0, 0, axis_index_groups=front_list)  10.4 us
    all_to_all x1, starting transfers between devices, body(): recv = lax.all_to_all(send, 'light', 0, 0, axis_index_groups=cells_list)  8.12 us
    ppermute x1, starting transfers between devices, body(): low = lax.ppermute(last, 'light', [(i, i + 1) for i in range(ends)])  3.08 us
    pallas_call x1, Pallas kernels, body(): fronts = propagate(in_vmem(recv), in_vmem(light_rows), const)  2.18 us
    pallas_call x1, Pallas kernels, body(): pl.pallas_call(local_kernel, out_shape=(out((layers, rows, S, T), F32), o...  2.02 us
    pallas_call x1, Pallas kernels, body(): pl.pallas_call(lambda *refs: prepare_kernel(*refs, total_y=rows * views),...  1.74 us
    ppermute x1, starting transfers between devices, body(): high = lax.ppermute(first, 'light', [(i + 1, i) for i in range(ends)])  1.29 us
  transfers between devices with their start and end apart: 3, of which 1 were waited for; matrix products, arithmetic and copies ran while one was open for 1% of the time, Pallas kernels for 7%

profile of v7, /device:TPU:1, one launch (start us, length us, event | category | flops | bytes accessed | tf_op | source)
XLA Modules:
  0.0 56.2 jit_solution(17417622790851421538)
XLA Ops:
  0.7 1.7 %prepare.1 = (bf16[4,16,8,256]{3,2,1,0:T(8,128)(2,1)S(1)}, f32[22,8,128]{2,1,0:T(8,128)S(1)}, bf16[8,4,2,8,256]{4,3,2,1,0:T(8,128)(2,1)}) custom-call(bf16[4,16,2048]{2,1,0:T(8,128)(2,1)} %refs_0_.1, s32[1,1,16]{2,1,0:T(1,128)} %refs_1_.1, f32[4,4]{1,0:T(4,128)} %refs_2_.1, f32[3]{0:T(128)} %refs_3_.1, f32[1]{0:T(128)S(6)} %copy.7.refs_4_.sign_ref), custom_call_target="tpu_custom_call" | custom-call | tf_op jit(solution)/shard_map/prepare/pallas_call | solution.py:313
  2.4 8.1 %all-to-all-start = ((bf16[8,4,2,8,256]{4,3,2,1,0:T(8,128)(2,1)}), bf16[8,4,2,8,256]{4,3,2,1,0:T(8,128)(2,1)S(1)}, u32[]{:S(2)}, u32[]{:S(2)}) async-start(bf16[8,4,2,8,256]{4,3,2,1,0:T(8,128)(2,1)} %get-tuple-element.16), calls=%async_computation | async-start | bytes 524288 | tf_op jit(solution)/shard_map/all_to_all | solution.py:344
  10.5 0.7 %slice_bitcast_fusion = (bf16[16,8,256]{2,1,0:T(8,128)(2,1)}, bf16[16,8,256]{2,1,0:T(8,128)(2,1)}) fusion(bf16[4,16,8,256]{3,2,1,0:T(8,128)(2,1)S(1)} %get-tuple-element.17.cells_ref), kind=kLoop, calls=%fused_computation | loop fusion | bytes 262144 | tf_op jit(solution)/shard_map/squeeze | solution.py:341
  11.2 3.1 %collective-permute-start = (bf16[16,8,256]{2,1,0:T(8,128)(2,1)}, bf16[16,8,256]{2,1,0:T(8,128)(2,1)S(1)}, u32[]{:S(2)}, u32[]{:S(2)}) collective-permute-start(bf16[16,8,256]{2,1,0:T(8,128)(2,1)} %get-tuple-element.28), channel_id=1, source_target_pairs={{0,64},{64,128},{128,192},{192,256},{256,320},{320,384},{384,448},... | collective-permute-start | bytes 196616 | tf_op jit(solution)/shard_map/ppermute | solution.py:342
  14.3 1.3 %collective-permute-start.1 = (bf16[16,8,256]{2,1,0:T(8,128)(2,1)}, bf16[16,8,256]{2,1,0:T(8,128)(2,1)S(1)}, u32[]{:S(2)}, u32[]{:S(2)}) collective-permute-start(bf16[16,8,256]{2,1,0:T(8,128)(2,1)} %get-tuple-element.27), channel_id=1, source_target_pairs={{64,0},{128,64},{192,128},{256,192},{320,256},{384,320},{448,384},... | collective-permute-start | bytes 196616 | tf_op jit(solution)/shard_map/ppermute | solution.py:343
  15.6 2.0 %local.1 = (f32[4,16,8,256]{3,2,1,0:T(8,128)S(1)}, f32[4,16,3,8,256]{4,3,2,1,0:T(8,128)S(1)}, f32[2,2,16,8,256]{4,3,2,1,0:T(8,128)S(1)}, f32[4,4,8,256]{3,2,1,0:T(8,128)S(1)}, f32[3,2,8,256]{3,2,1,0:T(8,128)S(1)}) custom-call(bf16[4,16,8,256]{3,2,1,0:T(8,128)(2,1)S(1)} %get-tuple-element.17.cells_ref, f32[3,16,2048]{2,1,0:T(8,128)} %light_ref.1, ...), custom_call_target="tpu_custom_call" | custom-call | tf_op jit(solution)/shard_map/local/pallas_call | solution.py:346
  17.6 0.0 all-to-all-done.recv_ref
  17.6 2.2 %propagate.1 = bf16[8,3,2,8,256]{4,3,2,1,0:T(8,128)(2,1)S(1)} custom-call(bf16[8,4,2,8,256]{4,3,2,1,0:T(8,128)(2,1)S(1)} %all-to-all-done.recv_ref, f32[3,2,8,256]{3,2,1,0:T(8,128)S(1)} %get-tuple-element.19.rows_ref, f32[22,8,128]{2,1,0:T(8,128)S(1)} %get-tuple-element.18.const_ref), custom_call_target="tpu_custom_call" | custom-call | tf_op jit(solution)/shard_map/propagate/pallas_call | solution.py:370
  19.8 0.0 collective-permute-done.low_ref
  19.8 0.7 %collective-permute-done.1.high_ref = bf16[16,8,256]{2,1,0:T(8,128)(2,1)S(1)} collective-permute-done((bf16[16,8,256]{2,1,0:T(8,128)(2,1)}, bf16[16,8,256]{2,1,0:T(8,128)(2,1)S(1)}, u32[]{:S(2)}, u32[]{:S(2)}) %collective-permute-start.1) | collective-permute-done | bytes 65568 | tf_op jit(solution)/shard_map/ppermute | solution.py:343
  20.5 10.4 %all_to_all.15.front_ref = bf16[8,3,2,8,256]{4,3,2,1,0:T(8,128)(2,1)S(1)} all-to-all(bf16[8,3,2,8,256]{4,3,2,1,0:T(8,128)(2,1)S(1)} %propagate.1), channel_id=1, replica_groups={{256,320,384,448,0,64,128,192},{257,321,385,449,1,65,129,193},{258,322,..., dimensions={0} | all-to-all | bytes 393216 | tf_op jit(solution)/shard_map/all_to_all | solution.py:372
  31.0 1.1 %shade.1 = f32[256,128]{1,0:T(8,128)S(1)} custom-call(bf16[8,3,2,8,256]{4,3,2,1,0:T(8,128)(2,1)S(1)} %all_to_all.15.front_ref, bf16[16,8,256]{2,1,0:T(8,128)(2,1)S(1)} %collective-permute-done.low_ref, bf16[16,8,256]{2,1,0:T(8,128)(2,1)S(1)} %collective-permute-done.1.high_ref, bf16[4,16,8,256]{3,2,1,0:T(8,128)(2,1)S(1)} %get-tuple-element.17.cells_ref, ...), custom_call_target="tpu_custom_call" | custom-call | tf_op jit(solution)/shard_map/shade/pallas_call | solution.py:374
  32.1 23.5 %all_to_all.16 = f32[64,4,128]{2,1,0:T(4,128)S(1)} all-to-all(f32[64,4,128]{2,1,0:T(4,128)S(1)} %bitcast.6), channel_id=1, replica_groups={{61,60,59,58,57,56,55,54,53,52,51,50,49,48,47,46,45,44,43,42,41,40,39,3..., dimensions={0} | all-to-all | bytes 262144 | tf_op jit(solution)/shard_map/all_to_all | solution.py:384
  55.5 0.7 %merge.1 = f32[4,128]{1,0:T(4,128)} custom-call(f32[256,128]{1,0:T(8,128)S(1)} %bitcast.7, f32[1]{0:T(128)S(6)} %copy.7.refs_4_.sign_ref), custom_call_target="tpu_custom_call" | custom-call | tf_op jit(solution)/shard_map/merge/pallas_call | solution.py:386
Async XLA Ops:
  2.4 15.2 %all-to-all-start = ((bf16[8,4,2,8,256]{4,3,2,1,0:T(8,128)(2,1)}), bf16[8,4,2,8,256]{4,3,2,1,0:T(8,128)(2,1)S(1)}, u32[]{:S(2)}, u32[]{:S(2)}) async-start(bf16[8,4,2,8,256]{4,3,2,1,0:T(8,128)(2,1)} %get-tuple-element.16), calls=%async_computation | async-start | bytes 524288 | tf_op jit(solution)/shard_map/all_to_all | solution.py:344
  11.2 8.6 %collective-permute-start = (bf16[16,8,256]{2,1,0:T(8,128)(2,1)}, bf16[16,8,256]{2,1,0:T(8,128)(2,1)S(1)}, u32[]{:S(2)}, u32[]{:S(2)}) collective-permute-start(bf16[16,8,256]{2,1,0:T(8,128)(2,1)} %get-tuple-element.28), channel_id=1, source_target_pairs={{0,64},{64,128},{128,192},{192,256},{256,320},{320,384},{384,448},... | collective-permute-start | bytes 196616 | tf_op jit(solution)/shard_map/ppermute | solution.py:342
  14.3 6.2 %collective-permute-start.1 = (bf16[16,8,256]{2,1,0:T(8,128)(2,1)}, bf16[16,8,256]{2,1,0:T(8,128)(2,1)S(1)}, u32[]{:S(2)}, u32[]{:S(2)}) collective-permute-start(bf16[16,8,256]{2,1,0:T(8,128)(2,1)} %get-tuple-element.27), channel_id=1, source_target_pairs={{64,0},{128,64},{192,128},{256,192},{320,256},{384,320},{448,384},... | collective-permute-start | bytes 196616 | tf_op jit(solution)/shard_map/ppermute | solution.py:343

commit v8 on v7

--- a/solution.py
+++ b/solution.py
@@ -75,8 +75,8 @@
 
 
 def prepare_kernel(
-    dens_ref, occ_hbm, transfer_hbm, absorb_hbm, sign_ref, cells_ref, const_ref, send_ref,
-    raw, packed, tmp, occ_ref, transfer_ref, absorb_ref, in_sem, out_sem, small_sem, *, total_y,
+    dens_ref, occ_hbm, transfer_hbm, absorb_hbm, light_hbm, sign_ref, cells_ref, const_ref, rows_ref, send_ref,
+    raw, packed, light, tmp, occ_ref, transfer_ref, absorb_ref, in_sem, out_sem, small_sem, light_sem, *, total_y,
 ):
     layers, rows, _ = dens_ref.shape
     small = [
@@ -87,7 +87,8 @@
     ]
     loads = [pltpu.make_async_copy(dens_ref.at[n], raw.at[n], in_sem.at[n]) for n in range(layers)]
     stores = [pltpu.make_async_copy(packed.at[:, n], send_ref.at[:, n], out_sem.at[n]) for n in range(layers)]
-    for copy in small[:1] + loads + small[1:]:
+    light_load = pltpu.make_async_copy(light_hbm, light, light_sem)
+    for copy in small[:1] + loads + small[1:] + [light_load]:
         copy.start()
     small[0].wait()
     occ = brick_mask(occ_ref)
@@ -115,6 +116,12 @@
     const_ref[PATH] = (2.0 / total_y) / jnp.abs(jnp.full((S, H), sign_ref[0], F32))
     for h in range(2):
         const_ref[OCCUPANCY + h] = occ[h]
+    light_load.wait()
+    start = 2 * lax.axis_index("light")
+    for c in range(3):
+        for r in range(2):
+            for s in range(S):
+                rows_ref[c, r, s : s + 1, :] = light[c, pl.ds(start + r, 1), (S - 1 - s) * T : (S - s) * T]
     for store in stores:
         store.wait()
 
@@ -157,12 +164,10 @@
 
 
 def local_kernel(
-    cells_ref, light_ref, const_ref, sign_ref,
-    ext_ref, gain_ref, slope_ref, base_ref, rows_ref, light, sem,
+    cells_ref, const_ref, sign_ref,
+    ext_ref, gain_ref, slope_ref, base_ref,
 ):
     layers, rows = cells_ref.shape[0], cells_ref.shape[1]
-    load = pltpu.make_async_copy(light_ref, light, sem)
-    load.start()
     occ = [const_ref[OCCUPANCY + h] for h in range(2)]
     back = sign_ref[0] < 0.0
     path = const_ref[PATH]
@@ -217,12 +222,6 @@
             for c in range(3):
                 base_ref[layer, c, :, h * H : (h + 1) * H] = 0.2 * base[h][c]
             base_ref[layer, 3, :, h * H : (h + 1) * H] = 1.0 - through[h]
-    load.wait()
-    start = 2 * lax.axis_index("light")
-    for c in range(3):
-        for r in range(2):
-            for s in range(S):
-                rows_ref[c, r, s : s + 1, :] = light[c, pl.ds(start + r, 1), (S - 1 - s) * T : (S - s) * T]
 
 
 def place(send_ref, layer, h, c, value):
@@ -310,27 +309,30 @@
     out = pltpu.VMEM
     small = (occupied, transfer, absorb)
 
-    cells, const, send = pl.pallas_call(
+    cells, const, light_rows, send = pl.pallas_call(
         lambda *refs: prepare_kernel(*refs, total_y=rows * views),
         out_shape=(
             out((layers, rows, S, T), BF16),
             out((PLANES, S, H), F32),
+            out((3, 2, S, T), F32),
             pltpu.HBM((lights, layers, 2, S, T), BF16),
         ),
-        in_specs=[ANY] * 4 + [SMEM],
-        out_specs=(VMEM, VMEM, ANY),
+        in_specs=[ANY] * 5 + [SMEM],
+        out_specs=(VMEM, VMEM, VMEM, ANY),
         scratch_shapes=[
             pltpu.VMEM((layers, rows, columns), BF16),
             pltpu.VMEM((lights, layers, 2, S, T), BF16),
+            pltpu.VMEM(light_in.shape, F32),
             pltpu.VMEM((layers, 2, rows * S, H), F32),
             *[pltpu.SMEM(x.shape, x.dtype) for x in small],
             pltpu.SemaphoreType.DMA((layers,)),
             pltpu.SemaphoreType.DMA((layers,)),
             pltpu.SemaphoreType.DMA((len(small),)),
+            pltpu.SemaphoreType.DMA(()),
         ],
         compiler_params=LIMIT,
         name="prepare",
-    )(*[in_hbm(x) for x in (density, *small)], view_sign)
+    )(*[in_hbm(x) for x in (density, *small, light_in)], view_sign)
     const = in_vmem(const)
 
     cells_list, front_list = [
@@ -343,21 +345,19 @@
     high = lax.ppermute(first, "light", [(i + 1, i) for i in range(ends)])
     recv = lax.all_to_all(send, "light", 0, 0, axis_index_groups=cells_list)
 
-    ext, gain, slope, base, light_rows = pl.pallas_call(
+    ext, gain, slope, base = pl.pallas_call(
         local_kernel,
         out_shape=(
             out((layers, rows, S, T), F32),
             out((layers, rows, 3, S, T), F32),
             out((2, 2, rows, S, T), F32),
             out((layers, 4, S, T), F32),
-            out((3, 2, S, T), F32),
         ),
-        in_specs=[VMEM, ANY, VMEM, SMEM],
-        out_specs=(VMEM,) * 5,
-        scratch_shapes=[pltpu.VMEM(light_in.shape, F32), pltpu.SemaphoreType.DMA(())],
+        in_specs=[VMEM, VMEM, SMEM],
+        out_specs=(VMEM,) * 4,
         compiler_params=LIMIT,
         name="local",
-    )(in_vmem(cells), in_hbm(light_in), const, view_sign)
+    )(in_vmem(cells), const, view_sign)
 
     propagate = pl.pallas_call(
         propagate_kernel,

time: 56.6 us -> 57.6 us (1.018)
  starting transfers between devices: 12.5 us -> 21.8 us
  blocking collectives: 33.9 us -> 24.8 us
  waiting for transfers between devices: 0.71 us -> 1.53 us
  Pallas kernels: 7.74 us -> 8.39 us
  local copies, waits for them, and re-layouts: 0.66 us -> 0.01 us
    all_to_all x1 -> x0, blocking collectives: 10.4 us -> none  [body(): front = lax.all_to_all(fronts, 'light', 0, 0, axis_index_groups=front_list)]
    all_to_all x0 -> x1, starting transfers between devices: none -> 8.4 us  [body(): front = lax.all_to_all(fronts, 'light', 0, 0, axis_index_groups=front_list)]
    all_to_all x0 -> x1, waiting for transfers between devices: none -> 1.52 us  [body(): front = lax.all_to_all(fronts, 'light', 0, 0, axis_index_groups=front_list)]
    all_to_all x1, blocking collectives: 23.5 us -> 24.8 us  [body(): lax.all_to_all(partial.reshape(views, 4, H), 'view', 0, 0, axis_index_gro...]
    ppermute x1, starting transfers between devices: 3.08 us -> 3.99 us  [body(): low = lax.ppermute(last, 'light', [(i, i + 1) for i in range(ends)])]
    ppermute x1, waiting for transfers between devices: 0.71 us -> 0.01 us  [body(): high = lax.ppermute(first, 'light', [(i + 1, i) for i in range(ends)])]
    pallas_call x1, Pallas kernels: 2.18 us -> 2.85 us  [body(): fronts = propagate(in_vmem(recv), in_vmem(light_rows), const)]
    squeeze x1, local copies, waits for them, and re-layouts: 0.66 us -> 0.01 us  [body(): first, last = (cells[0], cells[layers - 1])]
  transfers between devices with their start and end apart: 3 -> 4, of which waited for: 1 -> 1; matrix products, arithmetic and copies ran while one was open for 1% -> 0% of each run, Pallas kernels for 7% -> 9%
where the time goes in v8:
time: 57.6 us; the launch traced here: 57.2 us
  blocking collectives  24.8 us (43%)
  starting transfers between devices  21.8 us (38%)
  Pallas kernels  8.39 us (15%)
  waiting for transfers between devices  1.53 us (3%)
  between operations  0.71 us (1%)
    all_to_all x1, blocking collectives, body(): lax.all_to_all(partial.reshape(views, 4, H), 'view', 0, 0, axis_index_gro...  24.8 us
    all_to_all x1, starting transfers between devices, body(): front = lax.all_to_all(fronts, 'light', 0, 0, axis_index_groups=front_list)  8.4 us
    all_to_all x1, starting transfers between devices, body(): recv = lax.all_to_all(send, 'light', 0, 0, axis_index_groups=cells_list)  8.12 us
    ppermute x1, starting transfers between devices, body(): low = lax.ppermute(last, 'light', [(i, i + 1) for i in range(ends)])  3.99 us
    pallas_call x1, Pallas kernels, body(): fronts = propagate(in_vmem(recv), in_vmem(light_rows), const)  2.85 us
    pallas_call x1, Pallas kernels, body(): pl.pallas_call(local_kernel, out_shape=(out((layers, rows, S, T), F32), o...  2.01 us
    pallas_call x1, Pallas kernels, body(): pl.pallas_call(lambda *refs: prepare_kernel(*refs, total_y=rows * views),...  1.73 us
    all_to_all x1, waiting for transfers between devices, body(): front = lax.all_to_all(fronts, 'light', 0, 0, axis_index_groups=front_list)  1.52 us
  transfers between devices with their start and end apart: 4, of which 1 were waited for; matrix products, arithmetic and copies ran while one was open for 0% of the time, Pallas kernels for 9%

profile of v8, /device:TPU:1, one launch (start us, length us, event | category | flops | bytes accessed | tf_op | source)
XLA Modules:
  0.0 57.2 jit_solution(6100826095641009575)
XLA Ops:
  0.7 1.7 %prepare.1 = (bf16[4,16,8,256]{3,2,1,0:T(8,128)(2,1)S(1)}, f32[22,8,128]{2,1,0:T(8,128)S(1)}, f32[3,2,8,256]{3,2,1,0:T(8,128)S(1)}, bf16[8,4,2,8,256]{4,3,2,1,0:T(8,128)(2,1)}) custom-call(bf16[4,16,2048]{2,1,0:T(8,128)(2,1)} %refs_0_.1, s32[1,1,16]{2,1,0:T(1,128)} %refs_1_.1, f32[4,4]{1,0:T(4,128)} %refs_2_.1, f32[3]{0:T(128)} %refs_3_.1, ...), custom_call_target="tpu_custom_call" | custom-call | tf_op jit(solution)/shard_map/prepare/pallas_call | solution.py:312
  2.4 8.1 %all-to-all-start = ((bf16[8,4,2,8,256]{4,3,2,1,0:T(8,128)(2,1)}), bf16[8,4,2,8,256]{4,3,2,1,0:T(8,128)(2,1)S(1)}, u32[]{:S(2)}, u32[]{:S(2)}) async-start(bf16[8,4,2,8,256]{4,3,2,1,0:T(8,128)(2,1)} %get-tuple-element.16), calls=%async_computation | async-start | bytes 524288 | tf_op jit(solution)/shard_map/all_to_all | solution.py:346
  10.5 1.3 %collective-permute-start.1 = (bf16[16,8,256]{2,1,0:T(8,128)(2,1)S(1)}, bf16[16,8,256]{2,1,0:T(8,128)(2,1)S(1)}, u32[]{:S(2)}, u32[]{:S(2)}) collective-permute-start(bf16[16,8,256]{2,1,0:T(8,128)(2,1)S(1)} %get-tuple-element.27), channel_id=1, source_target_pairs={{64,0},{128,64},{192,128},{256,192},{320,256},{384,320},{448,384},... | collective-permute-start | bytes 196616 | tf_op jit(solution)/shard_map/ppermute | solution.py:345
  11.8 4.0 %collective-permute-start = (bf16[16,8,256]{2,1,0:T(8,128)(2,1)S(1)}, bf16[16,8,256]{2,1,0:T(8,128)(2,1)S(1)}, u32[]{:S(2)}, u32[]{:S(2)}) collective-permute-start(bf16[16,8,256]{2,1,0:T(8,128)(2,1)S(1)} %get-tuple-element.28), channel_id=1, source_target_pairs={{0,64},{64,128},{128,192},{192,256},{256,320},{320,384},{384,448},... | collective-permute-start | bytes 196616 | tf_op jit(solution)/shard_map/ppermute | solution.py:344
  15.8 0.0 all-to-all-done.recv_ref
  15.8 2.9 %propagate.1 = bf16[8,3,2,8,256]{4,3,2,1,0:T(8,128)(2,1)} custom-call(bf16[8,4,2,8,256]{4,3,2,1,0:T(8,128)(2,1)S(1)} %all-to-all-done.recv_ref, f32[3,2,8,256]{3,2,1,0:T(8,128)S(1)} %get-tuple-element.17.rows_ref, f32[22,8,128]{2,1,0:T(8,128)S(1)} %get-tuple-element.18.const_ref), custom_call_target="tpu_custom_call" | custom-call | tf_op jit(solution)/shard_map/propagate/pallas_call | solution.py:370
  18.7 0.0 collective-permute-done.1.high_ref
  18.7 0.0 collective-permute-done.low_ref
  18.7 8.4 %all-to-all-start.1 = ((bf16[8,3,2,8,256]{4,3,2,1,0:T(8,128)(2,1)}), bf16[8,3,2,8,256]{4,3,2,1,0:T(8,128)(2,1)S(1)}, u32[]{:S(2)}, u32[]{:S(2)}) async-start(bf16[8,3,2,8,256]{4,3,2,1,0:T(8,128)(2,1)} %propagate.1), calls=%async_computation.1 | async-start | bytes 393216 | tf_op jit(solution)/shard_map/all_to_all | solution.py:372
  27.1 2.0 %local.1 = (f32[4,16,8,256]{3,2,1,0:T(8,128)S(1)}, f32[4,16,3,8,256]{4,3,2,1,0:T(8,128)S(1)}, f32[2,2,16,8,256]{4,3,2,1,0:T(8,128)S(1)}, f32[4,4,8,256]{3,2,1,0:T(8,128)S(1)}) custom-call(bf16[4,16,8,256]{3,2,1,0:T(8,128)(2,1)S(1)} %get-tuple-element.19.cells_ref, f32[22,8,128]{2,1,0:T(8,128)S(1)} %get-tuple-element.18.const_ref, f32[1]{0:T(128)S(6)} %copy.7.refs_5_.sign_ref), custom_call_target="tpu_custom_call" | custom-call | tf_op jit(solution)/shard_map/local/pallas_call | solution.py:348
  29.1 1.5 %all-to-all-done.1.front_ref = bf16[8,3,2,8,256]{4,3,2,1,0:T(8,128)(2,1)S(1)} async-done(((bf16[8,3,2,8,256]{4,3,2,1,0:T(8,128)(2,1)}), bf16[8,3,2,8,256]{4,3,2,1,0:T(8,128)(2,1)S(1)}, u32[]{:S(2)}, u32[]{:S(2)}) %all-to-all-start.1) | async-done | bytes 196640 | tf_op jit(solution)/shard_map/all_to_all | solution.py:372
  30.6 1.1 %shade.1 = f32[256,128]{1,0:T(8,128)S(1)} custom-call(bf16[8,3,2,8,256]{4,3,2,1,0:T(8,128)(2,1)S(1)} %all-to-all-done.1.front_ref, bf16[16,8,256]{2,1,0:T(8,128)(2,1)S(1)} %collective-permute-done.low_ref, bf16[16,8,256]{2,1,0:T(8,128)(2,1)S(1)} %collective-permute-done.1.high_ref, bf16[4,16,8,256]{3,2,1,0:T(8,128)(2,1)S(1)} %get-tuple-element.19.cells_ref, ...), custom_call_target="tpu_custom_call" | custom-call | tf_op jit(solution)/shard_map/shade/pallas_call | solution.py:374
  31.8 24.8 %all_to_all.15 = f32[64,4,128]{2,1,0:T(4,128)S(1)} all-to-all(f32[64,4,128]{2,1,0:T(4,128)S(1)} %bitcast.6), channel_id=1, replica_groups={{61,60,59,58,57,56,55,54,53,52,51,50,49,48,47,46,45,44,43,42,41,40,39,3..., dimensions={0} | all-to-all | bytes 262144 | tf_op jit(solution)/shard_map/all_to_all | solution.py:384
  56.5 0.7 %merge.1 = f32[4,128]{1,0:T(4,128)} custom-call(f32[256,128]{1,0:T(8,128)S(1)} %bitcast.7, f32[1]{0:T(128)S(6)} %copy.7.refs_5_.sign_ref), custom_call_target="tpu_custom_call" | custom-call | tf_op jit(solution)/shard_map/merge/pallas_call | solution.py:386
  (1 shorter events, 0.0 us)
Async XLA Ops:
  2.4 13.4 %all-to-all-start = ((bf16[8,4,2,8,256]{4,3,2,1,0:T(8,128)(2,1)}), bf16[8,4,2,8,256]{4,3,2,1,0:T(8,128)(2,1)S(1)}, u32[]{:S(2)}, u32[]{:S(2)}) async-start(bf16[8,4,2,8,256]{4,3,2,1,0:T(8,128)(2,1)} %get-tuple-element.16), calls=%async_computation | async-start | bytes 524288 | tf_op jit(solution)/shard_map/all_to_all | solution.py:346
  10.5 8.2 %collective-permute-start.1 = (bf16[16,8,256]{2,1,0:T(8,128)(2,1)S(1)}, bf16[16,8,256]{2,1,0:T(8,128)(2,1)S(1)}, u32[]{:S(2)}, u32[]{:S(2)}) collective-permute-start(bf16[16,8,256]{2,1,0:T(8,128)(2,1)S(1)} %get-tuple-element.27), channel_id=1, source_target_pairs={{64,0},{128,64},{192,128},{256,192},{320,256},{384,320},{448,384},... | collective-permute-start | bytes 196616 | tf_op jit(solution)/shard_map/ppermute | solution.py:345
  11.8 6.9 %collective-permute-start = (bf16[16,8,256]{2,1,0:T(8,128)(2,1)S(1)}, bf16[16,8,256]{2,1,0:T(8,128)(2,1)S(1)}, u32[]{:S(2)}, u32[]{:S(2)}) collective-permute-start(bf16[16,8,256]{2,1,0:T(8,128)(2,1)S(1)} %get-tuple-element.28), channel_id=1, source_target_pairs={{0,64},{64,128},{128,192},{192,256},{256,320},{320,384},{384,448},... | collective-permute-start | bytes 196616 | tf_op jit(solution)/shard_map/ppermute | solution.py:344
  18.7 11.9 %all-to-all-start.1 = ((bf16[8,3,2,8,256]{4,3,2,1,0:T(8,128)(2,1)}), bf16[8,3,2,8,256]{4,3,2,1,0:T(8,128)(2,1)S(1)}, u32[]{:S(2)}, u32[]{:S(2)}) async-start(bf16[8,3,2,8,256]{4,3,2,1,0:T(8,128)(2,1)} %propagate.1), calls=%async_computation.1 | async-start | bytes 393216 | tf_op jit(solution)/shard_map/all_to_all | solution.py:372
